TPU v7x, 32 devices: a whole 2x2x4 slice. The times are simulated.
32 devices in a mesh: rep: 1, fsdp: 32 (over z, y, x, core).
Axes of the slice: x: 2, y: 2, z: 4, core: 2. Of those that a mesh axis runs over, the one named last changes fastest.
Arguments:
- tokens: bfloat16 [24576, 4096], P(('rep', 'fsdp')), may hold values from -6 to 6
- cotangent: bfloat16 [24576, 512], P(('rep', 'fsdp')), may hold values from -0.0390625 to 0.0390625
- policy: float32 [4096, 512], P('fsdp'), may hold values from -0.09375 to 0.09375
- anchor: float32 [4096, 512], P('fsdp'), may hold values from -0.09375 to 0.09375
- moment: float32 [4096, 512], P('fsdp'), may hold values from -3 to 3
- second: float32 [4096, 512], P('fsdp'), may hold values from 0.25 to 4
- readout: float32 [512], replicated, may hold values from -6 to 6
- pair_index: int32 [64, 2], P(('rep', 'fsdp')), may hold values from 0 to 127, as said below
- noisy_flags: int32 [64], P(('rep', 'fsdp')), may hold values 0 or 1
Outputs:
- policy_next: float32 [4096, 512], P('fsdp')
- anchor_next: float32 [4096, 512], P('fsdp')
- moment_next: float32 [4096, 512], P('fsdp')
- second_next: float32 [4096, 512], P('fsdp')
- pair_loss: float32 [64], P(('rep', 'fsdp'))
Inputs may be any that keep to these rules, and one draw needn't show every extreme that they name: Each of the 128 sequences appears exactly once in pair_index.
All inputs are finite; a program needn't handle non-finite values. No bound on the sum of `noisy_flags` on one device may be relied on, other than what follows from the above.
Results may differ from a plain program's by a relative error of at most 0.0025.
Values may be sent and summed in bfloat16 or wider, within the bound.
A program may use at most 64 MiB of HBM per device.

v0:
```python
import functools
import itertools
import jax
import jax.numpy as jnp
from jax import lax
from jax.experimental import pallas as pl
from jax.experimental.pallas import tpu as pltpu
from jax.sharding import PartitionSpec as P

LEN = 192


beta_one = 0.9
beta_two = 0.95
step_count = 20
learn_rate = 0.003
adam_epsilon = 1e-08
blend_rate = 0.6
smoothing = 0.1


def adam_update(gradient, policy, anchor, moment, second):
    moment_new = beta_one * moment + (1.0 - beta_one) * gradient
    second_new = beta_two * second + (1.0 - beta_two) * gradient * gradient
    correct_one = 1.0 - beta_one**step_count
    correct_two = 1.0 - beta_two**step_count
    policy_new = policy - learn_rate * (moment_new / correct_one) / (
        jnp.sqrt(second_new / correct_two) + adam_epsilon
    )
    anchor_new = blend_rate * policy_new + (1.0 - blend_rate) * anchor
    return (policy_new, anchor_new, moment_new, second_new)


def token_scores(values, readout):
    return jnp.sum(jax.nn.log_sigmoid(values * readout[None, :]), axis=1)


def sequence_margin(policy_values, anchor_values, readout, sequence_length):
    token_gap = token_scores(policy_values, readout) - token_scores(anchor_values, readout)
    return jnp.mean(token_gap.reshape(-1, sequence_length), axis=1)


def pair_losses(margins, pair_index, noisy_flags):
    sequence_index = jnp.arange(margins.shape[0], dtype=jnp.int32)
    chosen = jnp.sum(
        jnp.where(pair_index[:, 0:1] == sequence_index[None, :], margins[None, :], 0.0), axis=1
    )
    rejected = jnp.sum(
        jnp.where(pair_index[:, 1:2] == sequence_index[None, :], margins[None, :], 0.0), axis=1
    )
    margin_gap = chosen - rejected
    logit_value = jnp.where(noisy_flags == 1, -margin_gap, margin_gap)
    return -(1.0 - smoothing) * jax.nn.log_sigmoid(logit_value) - smoothing * jax.nn.log_sigmoid(
        -logit_value
    )


def shards(tokens, cotangent, policy, anchor, moment, second, readout, pair_index, noisy_flags):
    part_sum = lax.psum_scatter(
        lax.dot_general(
            tokens, cotangent, (((0,), (0,)), ((), ())), preferred_element_type=jnp.float32
        ),
        "fsdp",
        scatter_dimension=0,
        tiled=True,
    )
    gradient = lax.psum(part_sum.astype(jnp.bfloat16), "rep").astype(jnp.float32)
    policy_next, anchor_next, moment_next, second_next = adam_update(
        gradient, policy, anchor, moment, second
    )
    policy_half = policy_next.astype(jnp.bfloat16)
    anchor_half = anchor_next.astype(jnp.bfloat16)
    policy_whole = lax.all_gather(policy_half, "fsdp", axis=0, tiled=True)
    anchor_whole = lax.all_gather(anchor_half, "fsdp", axis=0, tiled=True)
    policy_values = jnp.dot(tokens, policy_whole, preferred_element_type=jnp.float32)
    anchor_values = jnp.dot(tokens, anchor_whole, preferred_element_type=jnp.float32)
    margins_own = sequence_margin(policy_values, anchor_values, readout, LEN)
    all_margins = lax.all_gather(margins_own, ("rep", "fsdp"), axis=0, tiled=True)
    pair_loss = pair_losses(all_margins, pair_index, noisy_flags)
    return (policy_next, anchor_next, moment_next, second_next, pair_loss)


STEP_ORDER = (2, 1, 3, 0)
MESH_ID = pl.DeviceIdType.MESH


def fused_kernel(
    sizes,
    tokens,
    cotangent,
    policy,
    anchor,
    moment,
    second,
    readout,
    gradient_out,
    margin_out,
    tok,
    cot,
    cot_t,
    par,
    send_a1,
    recv_a1,
    keep_a,
    send_b1,
    recv_b1,
    keep_b,
    send_a2,
    recv_a2,
    send_b2,
    recv_b2,
    send_z,
    recv_z,
    grad_own,
    result,
    weights,
    acc,
    table,
    local_sem,
    swap_send,
    swap_recv,
    rs_send,
    rs_recv,
    out_send,
    out_recv,
    z_send,
    z_recv,
    g2_send,
    g2_recv,
    g3_send,
    g3_recv,
    m_send,
    m_recv,
):
    n, rows, tokens_own, half, depth, seq_own = sizes
    block = 2 * rows
    span = 4 * block
    low = half // 2
    me = lax.axis_index("fsdp")
    core = me % 2
    px = (me // 2) % 2
    py = (me // 4) % 2
    pz = me // 8
    chip = me // 2
    mate = me + 1 - 2 * core
    x_mate = me + 2 - 4 * px
    y_mate = me + 4 - 8 * py

    def z_mate(shift):
        return (me + 8 * shift) % n

    def remote(src, dst, send_sem, recv_sem, device):
        return pltpu.make_async_remote_copy(
            src_ref=src,
            dst_ref=dst,
            send_sem=send_sem,
            recv_sem=recv_sem,
            device_id={"fsdp": device},
            device_id_type=MESH_ID,
        )

    barrier = pltpu.get_barrier_semaphore()
    plane = [
        me + dc * (1 - 2 * core) + dx * (2 - 4 * px) + dy * (4 - 8 * py)
        for dc, dx, dy in itertools.product((0, 1), repeat=3)
    ][1:]
    others = plane + [z_mate(s) for s in (1, 2, 3)]
    for other in others:
        pl.semaphore_signal(barrier, inc=1, device_id={"fsdp": other}, device_id_type=MESH_ID)

    mine = pl.ds(pl.multiple_of(core * half, half), half)
    theirs = pl.ds(pl.multiple_of((1 - core) * half, half), half)
    params = (policy, anchor, moment, second)

    pair = 2 * block

    def columns(s, dy):
        start = ((pz + s) % 4) * span + ((py + dy) % 2) * pair
        return pl.ds(pl.multiple_of(start, pair), pair)

    pieces = [(s, dy) for s in STEP_ORDER for dy in (1, 0)]

    cot_local = pltpu.make_async_copy(cotangent.at[:, mine], cot.at[core], local_sem.at[4])
    cot_local.start()
    tok_local = {}
    for i, (s, dy) in enumerate(pieces):
        tok_local[s, dy] = pltpu.make_async_copy(
            tokens.at[:, columns(s, dy)], tok.at[core, :, columns(s, dy)], local_sem.at[10 + i]
        )
        tok_local[s, dy].start()
    par_local = []
    for a in range(4):
        copy = pltpu.make_async_copy(params[a].at[:, mine], par.at[a, core], local_sem.at[5 + a])
        copy.start()
        par_local.append(copy)

    pl.semaphore_wait(barrier, len(others))

    sends = []
    cot_swap = remote(cotangent.at[:, theirs], cot.at[core], swap_send.at[4], swap_recv.at[4], mate)
    cot_swap.start()
    sends.append(cot_swap)
    tok_swap = {}
    for i, (s, dy) in enumerate(pieces):
        tok_swap[s, dy] = remote(
            tokens.at[:, columns(s, dy)],
            tok.at[core, :, columns(s, dy)],
            swap_send.at[10 + i],
            swap_recv.at[10 + i],
            mate,
        )
        tok_swap[s, dy].start()
        sends.append(tok_swap[s, dy])
    par_swap = []
    for a in range(4):
        copy = remote(
            params[a].at[:, theirs], par.at[a, core], swap_send.at[5 + a], swap_recv.at[5 + a], mate
        )
        copy.start()
        par_swap.append(copy)
        sends.append(copy)

    cot_local.wait()
    cot_swap.wait_recv()
    for r in range(2):
        cot_t[:, r * tokens_own : (r + 1) * tokens_own] = (
            cot[r].astype(jnp.float32).T.astype(jnp.bfloat16)
        )

    def first(s, dy):
        tok_local[s, dy].wait()
        tok_swap[s, dy].wait_recv()

    def block_gradient(s, dy, dx):
        target = ((pz + s) % 4) * 4 + ((py + dy) % 2) * 2 + (px + dx) % 2
        where = pl.ds(pl.multiple_of(target * block, block), block)
        total = jnp.dot(
            cot_t[:, :tokens_own], tok[0, :, where], preferred_element_type=jnp.float32
        )
        total += jnp.dot(
            cot_t[:, tokens_own:], tok[1, :, where], preferred_element_type=jnp.float32
        )
        if dx == 1:
            send_a1[s, dy] = total[:low].astype(jnp.bfloat16)
        else:
            keep_a[s, dy] = total[:low]
        if dy == 1:
            send_b1[s, dx] = total[low:].astype(jnp.bfloat16)
        else:
            keep_b[s, dx] = total[low:]

    hops = {}

    def hop(name, s, slot, src, dst, device):
        copy = remote(src, dst, rs_send.at[slot, s], rs_recv.at[slot, s], device)
        copy.start()
        hops[name, s] = copy
        sends.append(copy)

    def stage_one(s):
        first(s, 1)
        block_gradient(s, 1, 1)
        block_gradient(s, 1, 0)
        hop("b1", s, 1, send_b1.at[s], recv_b1.at[s], y_mate)
        first(s, 0)
        block_gradient(s, 0, 1)
        hop("a1", s, 0, send_a1.at[s], recv_a1.at[s], x_mate)
        block_gradient(s, 0, 0)

    def stage_two(s):
        hops["a1", s].wait_recv()
        send_a2[s] = (keep_a[s, 1] + recv_a1[s, 1].astype(jnp.float32)).astype(jnp.bfloat16)
        hop("a2", s, 2, send_a2.at[s], recv_a2.at[s], y_mate)
        hops["b1", s].wait_recv()
        send_b2[s] = (keep_b[s, 1] + recv_b1[s, 1].astype(jnp.float32)).astype(jnp.bfloat16)
        hop("b2", s, 3, send_b2.at[s], recv_b2.at[s], x_mate)

    def stage_three(s):
        hops["a2", s].wait_recv()
        total_a = keep_a[s, 0] + recv_a1[s, 0].astype(jnp.float32) + recv_a2[s].astype(jnp.float32)
        hops["b2", s].wait_recv()
        total_b = keep_b[s, 0] + recv_b1[s, 0].astype(jnp.float32) + recv_b2[s].astype(jnp.float32)
        if s == 0:
            grad_own[:low] = total_a
            grad_own[low:] = total_b
        else:
            send_z[s - 1, :low] = total_a.astype(jnp.bfloat16)
            send_z[s - 1, low:] = total_b.astype(jnp.bfloat16)
            hop("z", s, 4, send_z.at[s - 1], recv_z.at[s - 1], z_mate(s))

    for i in range(len(STEP_ORDER) + 2):
        if i < len(STEP_ORDER):
            stage_one(STEP_ORDER[i])
        if 1 <= i <= len(STEP_ORDER):
            stage_two(STEP_ORDER[i - 1])
        if i >= 2:
            stage_three(STEP_ORDER[i - 2])

    for a in range(4):
        par_local[a].wait()
        par_swap[a].wait_recv()
    for s in STEP_ORDER[:3]:
        hops["z", s].wait_recv()
    gradient = grad_own[...]
    for s in range(3):
        gradient += recv_z[s].astype(jnp.float32)
    gradient = gradient.T
    home = chip * block
    for r in range(2):
        updated = adam_update(
            gradient[r * rows : (r + 1) * rows], par[0, r], par[1, r], par[2, r], par[3, r]
        )
        result[r] = gradient[r * rows : (r + 1) * rows]
        for m in range(2):
            weights[m, pl.ds(pl.multiple_of(home + r * rows, rows), rows), :] = updated[m].astype(
                jnp.bfloat16
            )

    top = pz // 2
    near = pz + top * (3 - 2 * pz)

    def source(t):
        there = (near, 1 - near, 2, 3)[t]
        return there + top * (3 - 2 * there)

    def part(m, k):
        return weights.at[m, pl.ds(pl.multiple_of(k * block, block), block), :]

    def z_copy(m, zz, way):
        ref = part(m, zz * 4 + py * 2 + px)
        device = z_mate(1) if way == 0 else z_mate(3)
        return remote(ref, ref, z_send.at[way, m, zz], z_recv.at[m, zz], device)

    def z_forward(zz, act):
        @pl.when(jnp.logical_and(zz <= pz, pz < 3))
        def _():
            for m in range(2):
                act(z_copy(m, zz, 0))

        @pl.when(jnp.logical_and(zz >= pz, pz > 0))
        def _():
            for m in range(2):
                act(z_copy(m, zz, 1))

    gathers = {}

    def gather_two(t, zz):
        for m in range(2):
            ref = part(m, zz * 4 + py * 2 + px)
            device = y_mate if m == 0 else x_mate
            copy = remote(ref, ref, g2_send.at[t, m], g2_recv.at[t, m], device)
            copy.start()
            gathers[2, t, m] = copy
            sends.append(copy)

    def gather_three(t, zz, late, m):
        ky = (py + late) % 2 if m == 0 else py
        kx = px if m == 0 else (px + late) % 2
        ref = part(m, zz * 4 + ky * 2 + kx)
        device = x_mate if m == 0 else y_mate
        copy = remote(ref, ref, g3_send.at[t, late, m], g3_recv.at[t, late, m], device)
        copy.start()
        gathers[3, t, late, m] = copy
        sends.append(copy)

    tile = tokens_own
    scale = readout[core]

    def score_sum(values):
        low_part = jnp.minimum(values, 0.0).reshape(LEN // 8, 8, half)
        factor = (1.0 + jnp.exp(-jnp.abs(values))).reshape(LEN // 8, 8, half)
        product = factor[0]
        for j in range(1, LEN // 8):
            product = product * factor[j]
        return jnp.sum(low_part, axis=0) - jnp.log(product)

    def arrived(t, late):
        for m in range(2):
            gathers[3, t, late, m].wait_recv()

    def compute(t, zz):
        where = pl.ds(pl.multiple_of(zz * span, span), span)

        @pl.loop(0, 2)
        def _(i):
            at = pl.ds(0, tile)
            lhs = tok[i, at, where]
            for m in range(2):
                value = jnp.dot(lhs, weights[m, where, :], preferred_element_type=jnp.float32)
                acc[m, i] = value if t == 0 else acc[m, i] + value

    def spot(zz, dy, dx):
        k = zz * 4 + ((py + dy) % 2) * 2 + (px + dx) % 2
        return pl.ds(pl.multiple_of(k * block, block), block)

    def compute_near(zz):
        @pl.loop(0, 2)
        def _(i):
            at = pl.ds(0, tile)
            for m in range(2):
                value = acc[m, i]
                for dy, dx in ((0, 0), (0, 1), (1, 0)):
                    where = spot(zz, dy, dx)
                    value += jnp.dot(
                        tok[i, at, where],
                        weights[m, where, :],
                        preferred_element_type=jnp.float32,
                    )
                acc[m, i] = value

    def compute_last(zz):
        where = spot(zz, 1, 1)

        @pl.loop(0, 2)
        def _(i):
            at = pl.ds(0, tile)
            lhs = tok[i, at, where]
            for m in range(2):
                value = jnp.dot(lhs, weights[m, where, :], preferred_element_type=jnp.float32)
                acc[m, i] = (value + acc[m, i]) * scale
            for j in range(tile // LEN):
                gap = score_sum(acc[0, i, j * LEN : (j + 1) * LEN]) - score_sum(
                    acc[1, i, j * LEN : (j + 1) * LEN]
                )
                gap = jnp.sum(gap, axis=0, keepdims=True)
                gap = jnp.sum(gap, axis=1, keepdims=True)
                table[core, chip, pl.ds(i * (tile // LEN) + j, 1), :] = jnp.broadcast_to(
                    gap * (1.0 / LEN), (1, 128)
                )

    waits = []
    for t in range(4):
        zz = source(t)
        if t > 0:
            for m in range(2):
                z_copy(m, zz, 0).wait_recv()
        z_forward(zz, lambda copy: copy.start())
        gather_two(t, zz)
        gather_three(t, zz, 0, 0)
        gather_three(t, zz, 0, 1)
        if t == 0:
            copy = pltpu.make_async_copy(result.at[core], gradient_out.at[:, mine], local_sem.at[9])
            copy.start()
            waits.append(copy)
            copy = remote(
                result.at[1 - core], gradient_out.at[:, mine], out_send.at[0], out_recv.at[0], mate
            )
            copy.start()
            waits.append(copy)
        for m in range(2):
            gathers[2, t, m].wait_recv()
            gather_three(t, zz, 1, m)
        if t > 0:
            arrived(t - 1, 0)
            arrived(t - 1, 1)
            compute(t - 1, source(t - 1))
    arrived(3, 0)
    compute_near(source(3))
    arrived(3, 1)
    compute_last(source(3))

    def table_copy(ref, slot, device):
        copy = remote(ref, ref, m_send.at[slot], m_recv.at[slot], device)
        copy.start()
        sends.append(copy)
        return copy

    near_copies = [
        table_copy(table.at[core, pl.ds(chip, 1)], i, device) for i, device in enumerate(plane)
    ]
    for copy in near_copies:
        copy.wait_recv()
    last = [
        table_copy(table.at[:, pl.ds(pz * 4, 4)], 6 + s, z_mate(s)) for s in (2, 1, 3)
    ]
    for copy in last:
        copy.wait_recv()
    for copy in waits:
        copy.wait()
    for copy in sends:
        copy.wait_send()
    for t in range(4):
        z_forward(source(t), lambda copy: copy.wait_send())
    margin_out[...] = table[...]


def finish_kernel(
    gradient,
    policy,
    anchor,
    moment,
    second,
    table,
    pair_index,
    noisy_flags,
    policy_out,
    anchor_out,
    moment_out,
    second_out,
    loss_out,
):
    updated = adam_update(gradient[...], policy[...], anchor[...], moment[...], second[...])
    for out, value in zip((policy_out, anchor_out, moment_out, second_out), updated):
        out[...] = value
    margins = table[0] + table[1]
    sequence = lax.broadcasted_iota(jnp.int32, margins.shape, 0)

    def margin_of(index):
        return jnp.sum(jnp.where(sequence == index, margins, 0.0), axis=0, keepdims=True)

    for p in range(noisy_flags.shape[0]):
        gap = margin_of(pair_index[p, 0]) - margin_of(pair_index[p, 1])
        gap = jnp.where(noisy_flags[p] == 1, -gap, gap)
        tail = jnp.log(1.0 + jnp.exp(-jnp.abs(gap)))
        loss = (1.0 - smoothing) * (tail - jnp.minimum(gap, 0.0)) + smoothing * (
            tail + jnp.maximum(gap, 0.0)
        )
        loss_out[p] = loss[0, 0]


def fused_shards(n, tokens, cotangent, policy, anchor, moment, second, readout, pair_index, noisy_flags):
    tokens_own, depth = tokens.shape
    rows, channels = policy.shape
    half = channels // 2
    block = 2 * rows
    low = half // 2
    seq_chip = 2 * tokens_own // LEN
    sizes = (n, rows, tokens_own, half, depth, seq_chip // 2)
    bf, f32 = jnp.bfloat16, jnp.float32
    vmem, dma = pltpu.VMEM, pltpu.SemaphoreType.DMA
    hbm = pl.BlockSpec(memory_space=pl.ANY)
    whole = pl.BlockSpec(memory_space=pltpu.VMEM)
    weight = jax.ShapeDtypeStruct((rows, channels), f32)
    gradient, table = pl.pallas_call(
        functools.partial(fused_kernel, sizes),
        out_shape=(weight, jax.ShapeDtypeStruct((2, n // 2, seq_chip, 128), f32)),
        in_specs=[hbm] * 6 + [whole],
        out_specs=(hbm, whole),
        scratch_shapes=[
            vmem((2, tokens_own, depth), bf),
            vmem((2, tokens_own, half), bf),
            vmem((half, 2 * tokens_own), bf),
            vmem((4, 2, rows, half), f32),
            vmem((4, 2, low, block), bf),
            vmem((4, 2, low, block), bf),
            vmem((4, 2, low, block), f32),
            vmem((4, 2, low, block), bf),
            vmem((4, 2, low, block), bf),
            vmem((4, 2, low, block), f32),
            vmem((4, low, block), bf),
            vmem((4, low, block), bf),
            vmem((4, low, block), bf),
            vmem((4, low, block), bf),
            vmem((3, half, block), bf),
            vmem((3, half, block), bf),
            vmem((half, block), f32),
            vmem((2, rows, half), f32),
            vmem((2, depth, half), bf),
            vmem((2, 2, tokens_own, half), f32),
            vmem((2, n // 2, seq_chip, 128), f32),
            dma((18,)),
            dma((18,)),
            dma((18,)),
            dma((5, 4)),
            dma((5, 4)),
            dma((1,)),
            dma((1,)),
            dma((2, 2, 4)),
            dma((2, 4)),
            dma((4, 2)),
            dma((4, 2)),
            dma((4, 2, 2)),
            dma((4, 2, 2)),
            dma((10,)),
            dma((10,)),
        ],
        compiler_params=pltpu.CompilerParams(
            collective_id=0, has_side_effects=True, vmem_limit_bytes=56 * 1024 * 1024
        ),
    )(
        tokens,
        cotangent,
        policy,
        anchor,
        moment,
        second,
        readout.reshape(2, 1, half),
    )
    smem = pl.BlockSpec(memory_space=pltpu.SMEM)
    policy_next, anchor_next, moment_next, second_next, pair_loss = pl.pallas_call(
        finish_kernel,
        out_shape=(weight,) * 4 + (jax.ShapeDtypeStruct(noisy_flags.shape, f32),),
        in_specs=[whole] * 6 + [smem] * 2,
        out_specs=(whole,) * 4 + (smem,),
    )(
        gradient,
        policy,
        anchor,
        moment,
        second,
        table.reshape(2, n // 2 * seq_chip, 128),
        pair_index,
        noisy_flags,
    )
    return (policy_next, anchor_next, moment_next, second_next, pair_loss)


def solution(mesh):
    placed = (
        P(("rep", "fsdp"), None),
        P(("rep", "fsdp"), None),
        P("fsdp", None),
        P("fsdp", None),
        P("fsdp", None),
        P("fsdp", None),
        P(),
        P(("rep", "fsdp"), None),
        P(("rep", "fsdp")),
    )
    n = mesh.shape["fsdp"]
    body = shards
    if mesh.shape["rep"] == 1 and n // 8 == len(STEP_ORDER):
        body = functools.partial(fused_shards, n)
    return jax.shard_map(
        body,
        mesh=mesh,
        in_specs=placed,
        out_specs=(
            P("fsdp", None),
            P("fsdp", None),
            P("fsdp", None),
            P("fsdp", None),
            P(("rep", "fsdp")),
        ),
        check_vma=False,
    )
```

profile of v0, /device:TPU:0, one launch (start us, length us, event | category | flops | bytes accessed | tf_op | source)
XLA Modules:
  0.0 87.5 jit_solution(13586398842082387919)
XLA Ops:
  0.6 84.2 %shard_map.128 = (f32[128,512]{1,0:T(8,128)}, f32[2,16,8,128]{3,2,1,0:T(8,128)}) custom-call(bf16[768,4096]{1,0:T(8,128)(2,1)} %tokens.1, bf16[768,512]{1,0:T(8,128)(2,1)} %cotangent.1, f32[128,512]{1,0:T(8,128)} %policy.3, f32[128,512]{1,0:T(8,128)} %anchor.3, f32[128,512]{1,0:T(8,128)} %moment.3, f32[128,512]{1,0:T(8,128)} %second.3, f32[2,1,256]{2,1,0:T(1,128)} %bitcast.3), custom_call_target="tpu_custom_call" | custom-call | tf_op jit(solution)/shard_map/pallas_call | solution.py:534
  84.8 2.7 %shard_map.129 = (f32[128,512]{1,0:T(8,128)}, f32[128,512]{1,0:T(8,128)}, f32[128,512]{1,0:T(8,128)}, f32[128,512]{1,0:T(8,128)}, f32[2]{0:T(128)}) custom-call(f32[128,512]{1,0:T(8,128)} %get-tuple-element.7.gradient, f32[128,512]{1,0:T(8,128)} %policy.3, f32[128,512]{1,0:T(8,128)} %anchor.3, f32[128,512]{1,0:T(8,128)} %moment.3, f32[128,512]{1,0:T(8,128)} %second.3, ...), custom_call_target="tpu_custom_call" | custom-call | tf_op jit(solution)/shard_map/pallas_call | solution.py:590
where the time goes:
time: 87.7 us; the launch traced here: 87.5 us
  Pallas kernels  86.9 us (99%)
    pallas_call x1, Pallas kernels, fused_shards(): pl.pallas_call(functools.partial(fused_kernel, sizes), out_shape=(weight,...  84.2 us
    pallas_call x1, Pallas kernels, fused_shards(): pl.pallas_call(finish_kernel, out_shape=(weight,) * 4 + (jax.ShapeDtypeSt...  2.67 us

commit v1 on v0

v1 whole, which is shorter than its diff:
```python
import functools
import itertools
import jax
import jax.numpy as jnp
from jax import lax
from jax.experimental import pallas as pl
from jax.experimental.pallas import tpu as pltpu
from jax.sharding import PartitionSpec as P

LEN = 192


beta_one = 0.9
beta_two = 0.95
step_count = 20
learn_rate = 0.003
adam_epsilon = 1e-08
blend_rate = 0.6
smoothing = 0.1


def adam_update(gradient, policy, anchor, moment, second):
    moment_new = beta_one * moment + (1.0 - beta_one) * gradient
    second_new = beta_two * second + (1.0 - beta_two) * gradient * gradient
    correct_one = 1.0 - beta_one**step_count
    correct_two = 1.0 - beta_two**step_count
    policy_new = policy - learn_rate * (moment_new / correct_one) / (
        jnp.sqrt(second_new / correct_two) + adam_epsilon
    )
    anchor_new = blend_rate * policy_new + (1.0 - blend_rate) * anchor
    return (policy_new, anchor_new, moment_new, second_new)


def token_scores(values, readout):
    return jnp.sum(jax.nn.log_sigmoid(values * readout[None, :]), axis=1)


def sequence_margin(policy_values, anchor_values, readout, sequence_length):
    token_gap = token_scores(policy_values, readout) - token_scores(anchor_values, readout)
    return jnp.mean(token_gap.reshape(-1, sequence_length), axis=1)


def pair_losses(margins, pair_index, noisy_flags):
    sequence_index = jnp.arange(margins.shape[0], dtype=jnp.int32)
    chosen = jnp.sum(
        jnp.where(pair_index[:, 0:1] == sequence_index[None, :], margins[None, :], 0.0), axis=1
    )
    rejected = jnp.sum(
        jnp.where(pair_index[:, 1:2] == sequence_index[None, :], margins[None, :], 0.0), axis=1
    )
    margin_gap = chosen - rejected
    logit_value = jnp.where(noisy_flags == 1, -margin_gap, margin_gap)
    return -(1.0 - smoothing) * jax.nn.log_sigmoid(logit_value) - smoothing * jax.nn.log_sigmoid(
        -logit_value
    )


def shards(tokens, cotangent, policy, anchor, moment, second, readout, pair_index, noisy_flags):
    part_sum = lax.psum_scatter(
        lax.dot_general(
            tokens, cotangent, (((0,), (0,)), ((), ())), preferred_element_type=jnp.float32
        ),
        "fsdp",
        scatter_dimension=0,
        tiled=True,
    )
    gradient = lax.psum(part_sum.astype(jnp.bfloat16), "rep").astype(jnp.float32)
    policy_next, anchor_next, moment_next, second_next = adam_update(
        gradient, policy, anchor, moment, second
    )
    policy_half = policy_next.astype(jnp.bfloat16)
    anchor_half = anchor_next.astype(jnp.bfloat16)
    policy_whole = lax.all_gather(policy_half, "fsdp", axis=0, tiled=True)
    anchor_whole = lax.all_gather(anchor_half, "fsdp", axis=0, tiled=True)
    policy_values = jnp.dot(tokens, policy_whole, preferred_element_type=jnp.float32)
    anchor_values = jnp.dot(tokens, anchor_whole, preferred_element_type=jnp.float32)
    margins_own = sequence_margin(policy_values, anchor_values, readout, LEN)
    all_margins = lax.all_gather(margins_own, ("rep", "fsdp"), axis=0, tiled=True)
    pair_loss = pair_losses(all_margins, pair_index, noisy_flags)
    return (policy_next, anchor_next, moment_next, second_next, pair_loss)


PLANES = 4
EARLY = 64
MESH_ID = pl.DeviceIdType.MESH


def policy_update(gradient, policy, moment, second):
    moment_new = beta_one * moment + (1.0 - beta_one) * gradient
    second_new = beta_two * second + (1.0 - beta_two) * gradient * gradient
    correct_one = 1.0 - beta_one**step_count
    correct_two = 1.0 - beta_two**step_count
    return policy - learn_rate * (moment_new / correct_one) / (
        jnp.sqrt(second_new / correct_two) + adam_epsilon
    )


def fused_kernel(
    sizes,
    tokens,
    cotangent,
    policy,
    anchor,
    moment,
    second,
    readout,
    gradient_out,
    margin_out,
    tok,
    cot,
    cot_t,
    anc,
    anc_send,
    par,
    send_a1,
    recv_a1,
    keep_a,
    send_b1,
    recv_b1,
    keep_b,
    send_a2,
    recv_a2,
    send_b2,
    recv_b2,
    send_z,
    recv_z,
    grad_own,
    result,
    weights,
    acc,
    table,
    local_sem,
    swap_send,
    swap_recv,
    rs_send,
    rs_recv,
    rz_send,
    rz_recv,
    out_send,
    out_recv,
    xy_send,
    xy_recv,
    z_send,
    z_recv,
    m_send,
    m_recv,
):
    n, rows, tokens_own, half = sizes
    block = 2 * rows
    span = 4 * block
    pair = 2 * block
    low = half // 2
    me = lax.axis_index("fsdp")
    core = me % 2
    px = (me // 2) % 2
    py = (me // 4) % 2
    pz = me // 8
    chip = me // 2
    mate = me + 1 - 2 * core
    x_mate = me + 2 - 4 * px
    y_mate = me + 4 - 8 * py
    home = chip * block

    top = pz // 2
    near = pz + top * (3 - 2 * pz)

    def plane(t):
        there = (near, 1 - near, 2, 3)[t]
        return there + top * (3 - 2 * there)

    def z_mate(t):
        return me + 8 * (plane(t) - pz)

    def remote(src, dst, send_sem, recv_sem, device):
        return pltpu.make_async_remote_copy(
            src_ref=src,
            dst_ref=dst,
            send_sem=send_sem,
            recv_sem=recv_sem,
            device_id={"fsdp": device},
            device_id_type=MESH_ID,
        )

    barrier = pltpu.get_barrier_semaphore()
    others = [mate, x_mate, y_mate] + [z_mate(t) for t in (1, 2, 3)]
    for other in others:
        pl.semaphore_signal(barrier, inc=1, device_id={"fsdp": other}, device_id_type=MESH_ID)

    mine = pl.ds(pl.multiple_of(core * half, half), half)
    theirs = pl.ds(pl.multiple_of((1 - core) * half, half), half)
    params = (policy, moment, second)

    def columns(i, dy):
        start = plane(3 - i) * span + ((py + dy) % 2) * pair
        return pl.ds(pl.multiple_of(start, pair), pair)

    pieces = [(i, dy) for i in range(PLANES) for dy in (1, 0)]

    anc_local = []
    for r, side in enumerate((mine, theirs)):
        copy = pltpu.make_async_copy(anchor.at[:, side], anc.at[r], local_sem.at[r])
        copy.start()
        anc_local.append(copy)
    cot_local = pltpu.make_async_copy(cotangent.at[:, mine], cot.at[core], local_sem.at[2])
    cot_local.start()
    tok_local = {}
    for j, key in enumerate(pieces):
        where = columns(*key)
        tok_local[key] = pltpu.make_async_copy(
            tokens.at[:, where], tok.at[core, :, where], local_sem.at[8 + j]
        )
        tok_local[key].start()
    par_local = []
    for a in range(3):
        copy = pltpu.make_async_copy(params[a].at[:, mine], par.at[a, core], local_sem.at[3 + a])
        copy.start()
        par_local.append(copy)

    own_rows = pl.ds(pl.multiple_of(home + core * rows, rows), rows)
    anc_local[0].wait()
    weights[1, own_rows, :] = anc[0].astype(jnp.bfloat16)
    anc_local[1].wait()
    anc_send[...] = anc[1].astype(jnp.bfloat16)

    pl.semaphore_wait(barrier, len(others))

    sends = []

    def chip_at(zz, dy, dx):
        return zz * 4 + ((py + dy) % 2) * 2 + (px + dx) % 2

    kinds = {
        "c": (1, core * (block - EARLY), EARLY),
        "b": (1, (1 - core) * EARLY, block - EARLY),
        "p": (0, 0, block),
    }

    def part(kind, k, which=None):
        m, start, count = kinds[kind]
        if which is not None:
            count = count // 2
            start = start + which * count
        return weights.at[m, pl.ds(pl.multiple_of(k * block + start, 16), count), :]

    flights = {}

    def launch(name, copy):
        copy.start()
        flights[name] = copy
        sends.append(copy)

    def spread(kind, q, zz):
        ref = part(kind, chip_at(zz, 0, 0))
        launch((q, 0), remote(ref, ref, xy_send.at[q, 0], xy_recv.at[q, 0], x_mate))
        launch((q, 1), remote(ref, ref, xy_send.at[q, 1], xy_recv.at[q, 1], y_mate))

    def relay(kind, q, zz):
        flights[q, 1].wait_recv()
        ref = part(kind, chip_at(zz, 1, 0), 0)
        launch((q, 2), remote(ref, ref, xy_send.at[q, 2], xy_recv.at[q, 2], x_mate))
        flights[q, 0].wait_recv()
        ref = part(kind, chip_at(zz, 0, 1), 1)
        launch((q, 3), remote(ref, ref, xy_send.at[q, 3], xy_recv.at[q, 3], y_mate))

    def relayed(q):
        flights[q, 2].wait_recv()
        flights[q, 3].wait_recv()

    def z_out(kind, q, k):
        for t in (1, 2, 3):
            ref = part(kind, k)
            copy = remote(ref, ref, z_send.at[q, t - 1], z_recv.at[q, pz], z_mate(t))
            copy.start()
            sends.append(copy)

    def z_in(kind, q, t, dy=0, dx=0):
        ref = part(kind, chip_at(plane(t), dy, dx))
        remote(ref, ref, z_send.at[q, t - 1], z_recv.at[q, plane(t)], z_mate(t)).wait_recv()

    spread("c", 0, pz)
    z_out("c", 0, chip)
    launch(
        "anc",
        remote(anc_send, weights.at[1, own_rows, :], swap_send.at[0], swap_recv.at[0], mate),
    )
    cot_swap = remote(cotangent.at[:, theirs], cot.at[core], swap_send.at[1], swap_recv.at[1], mate)
    cot_swap.start()
    sends.append(cot_swap)
    tok_swap = {}
    for j, key in enumerate(pieces):
        where = columns(*key)
        tok_swap[key] = remote(
            tokens.at[:, where],
            tok.at[core, :, where],
            swap_send.at[8 + j],
            swap_recv.at[8 + j],
            mate,
        )
        tok_swap[key].start()
        sends.append(tok_swap[key])
    par_swap = []
    for a in range(3):
        copy = remote(
            params[a].at[:, theirs], par.at[a, core], swap_send.at[2 + a], swap_recv.at[2 + a], mate
        )
        copy.start()
        par_swap.append(copy)
        sends.append(copy)

    flights["anc"].wait_recv()
    z_out("b", 4, chip)
    spread("b", 1, pz)

    cot_local.wait()
    cot_swap.wait_recv()
    for r in range(2):
        cot_t[:, r * tokens_own : (r + 1) * tokens_own] = (
            cot[r].astype(jnp.float32).T.astype(jnp.bfloat16)
        )

    def first(key):
        tok_local[key].wait()
        tok_swap[key].wait_recv()

    def block_gradient(i, dy, dx):
        target = chip_at(plane(3 - i), dy, dx)
        where = pl.ds(pl.multiple_of(target * block, block), block)
        total = jnp.dot(
            cot_t[:, :tokens_own], tok[0, :, where], preferred_element_type=jnp.float32
        )
        total += jnp.dot(
            cot_t[:, tokens_own:], tok[1, :, where], preferred_element_type=jnp.float32
        )
        if dx == 1:
            send_a1[i, dy] = total[:low].astype(jnp.bfloat16)
        else:
            keep_a[i, dy] = total[:low]
        if dy == 1:
            send_b1[i, dx] = total[low:].astype(jnp.bfloat16)
        else:
            keep_b[i, dx] = total[low:]

    hops = {}

    def hop(name, i, slot, src, dst, device):
        copy = remote(src, dst, rs_send.at[slot, i], rs_recv.at[slot, i], device)
        copy.start()
        hops[name, i] = copy
        sends.append(copy)

    def send_b(i):
        hop("b1", i, 1, send_b1.at[i], recv_b1.at[i], y_mate)

    def send_a(i):
        hop("a1", i, 0, send_a1.at[i], recv_a1.at[i], x_mate)

    def stage_one(i, hold=False, between=None):
        first((i, 1))
        block_gradient(i, 1, 1)
        block_gradient(i, 1, 0)
        if not hold:
            send_b(i)
        if between is not None:
            between()
        first((i, 0))
        block_gradient(i, 0, 1)
        if not hold:
            send_a(i)
        block_gradient(i, 0, 0)

    def stage_two(i):
        hops["a1", i].wait_recv()
        send_a2[i] = (keep_a[i, 1] + recv_a1[i, 1].astype(jnp.float32)).astype(jnp.bfloat16)
        hop("a2", i, 2, send_a2.at[i], recv_a2.at[i], y_mate)
        hops["b1", i].wait_recv()
        send_b2[i] = (keep_b[i, 1] + recv_b1[i, 1].astype(jnp.float32)).astype(jnp.bfloat16)
        hop("b2", i, 3, send_b2.at[i], recv_b2.at[i], x_mate)

    def stage_three(i):
        hops["a2", i].wait_recv()
        total_a = keep_a[i, 0] + recv_a1[i, 0].astype(jnp.float32) + recv_a2[i].astype(jnp.float32)
        hops["b2", i].wait_recv()
        total_b = keep_b[i, 0] + recv_b1[i, 0].astype(jnp.float32) + recv_b2[i].astype(jnp.float32)
        if i == PLANES - 1:
            grad_own[:low] = total_a
            grad_own[low:] = total_b
        else:
            send_z[i, :low] = total_a.astype(jnp.bfloat16)
            send_z[i, low:] = total_b.astype(jnp.bfloat16)
            copy = remote(
                send_z.at[i], recv_z.at[pz], rz_send.at[i], rz_recv.at[pz], z_mate(3 - i)
            )
            copy.start()
            sends.append(copy)

    def early_out():
        relay("c", 0, pz)
        z_out("c", 1, chip_at(pz, 0, 1))
        z_out("c", 2, chip_at(pz, 1, 0))

    def blend_spread(t):
        z_in("b", 4, t)
        spread("b", 1 + t, plane(t))

    def blend_relay(t):
        relay("b", 1 + t, plane(t))

    stage_one(0, between=early_out)
    stage_one(1)
    blend_relay(0)
    stage_one(2)
    stage_two(0)
    stage_two(1)
    stage_one(3, hold=True)
    stage_two(2)
    send_b(3)
    send_a(3)
    stage_three(0)
    stage_three(1)
    blend_spread(1)
    stage_three(2)
    relayed(0)
    z_out("c", 3, chip_at(pz, 1, 1))
    stage_two(3)
    blend_relay(1)
    blend_spread(2)
    for a in range(3):
        par_local[a].wait()
        par_swap[a].wait_recv()
    for t in (3, 2, 1):
        zz = plane(t)
        remote(
            send_z.at[0], recv_z.at[zz], rz_send.at[0], rz_recv.at[zz], z_mate(t)
        ).wait_recv()
    stage_three(3)
    gradient = grad_own[...]
    for t in (1, 2, 3):
        gradient += recv_z[plane(t)].astype(jnp.float32)
    gradient = gradient.T
    for r in range(2):
        own = gradient[r * rows : (r + 1) * rows]
        updated = policy_update(own, par[0, r], par[1, r], par[2, r])
        result[r] = own
        weights[0, pl.ds(pl.multiple_of(home + r * rows, rows), rows), :] = updated.astype(
            jnp.bfloat16
        )
    z_out("p", 5, chip)
    spread("p", 5, pz)

    tile = tokens_own
    scale = readout[core]

    def score_sum(values):
        low_part = jnp.minimum(values, 0.0).reshape(LEN // 8, 8, half)
        factor = (1.0 + jnp.exp(-jnp.abs(values))).reshape(LEN // 8, 8, half)
        product = factor[0]
        for j in range(1, LEN // 8):
            product = product * factor[j]
        return jnp.sum(low_part, axis=0) - jnp.log(product)

    def multiply(m, t):
        where = pl.ds(pl.multiple_of(plane(t) * span, span), span)

        @pl.loop(0, 2)
        def _(i):
            value = jnp.dot(
                tok[i, :, where], weights[m, where, :], preferred_element_type=jnp.float32
            )
            acc[m, i] = value if t == 0 else acc[m, i] + value

    def anchor_multiply(t):
        relayed(1 + t)
        if t > 0:
            for j, (dy, dx) in enumerate(((0, 0), (0, 1), (1, 0), (1, 1))):
                z_in("c", j, t, dy, dx)
        multiply(1, t)

    def policy_multiply(t):
        relayed(5 + t)
        multiply(0, t)

    def policy_spread(t):
        z_in("p", 5, t)
        spread("p", 5 + t, plane(t))

    def policy_relay(t):
        relay("p", 5 + t, plane(t))

    def spot(zz, dy, dx):
        return pl.ds(pl.multiple_of(chip_at(zz, dy, dx) * block, block), block)

    def compute_near(zz):
        @pl.loop(0, 2)
        def _(i):
            value = acc[0, i]
            for dy, dx in ((0, 0), (0, 1), (1, 0)):
                where = spot(zz, dy, dx)
                value += jnp.dot(
                    tok[i, :, where], weights[0, where, :], preferred_element_type=jnp.float32
                )
            acc[0, i] = value

    def compute_last(zz):
        where = spot(zz, 1, 1)

        @pl.loop(0, 2)
        def _(i):
            value = acc[0, i] + jnp.dot(
                tok[i, :, where], weights[0, where, :], preferred_element_type=jnp.float32
            )
            acc[1, i] = (blend_rate * value + (1.0 - blend_rate) * acc[1, i]) * scale
            acc[0, i] = value * scale
            for j in range(tile // LEN):
                gap = score_sum(acc[0, i, j * LEN : (j + 1) * LEN]) - score_sum(
                    acc[1, i, j * LEN : (j + 1) * LEN]
                )
                gap = jnp.sum(gap, axis=0, keepdims=True)
                gap = jnp.sum(gap, axis=1, keepdims=True)
                table[core, chip, pl.ds(i * (tile // LEN) + j, 1), :] = jnp.broadcast_to(
                    gap * (1.0 / LEN), (1, 128)
                )

    waits = []
    copy = pltpu.make_async_copy(result.at[core], gradient_out.at[:, mine], local_sem.at[6])
    copy.start()
    waits.append(copy)
    copy = remote(
        result.at[1 - core], gradient_out.at[:, mine], out_send.at[0], out_recv.at[0], mate
    )
    copy.start()
    waits.append(copy)

    blend_relay(2)
    blend_spread(3)
    anchor_multiply(0)
    anchor_multiply(1)
    policy_relay(0)
    policy_spread(1)
    blend_relay(3)
    anchor_multiply(2)
    policy_spread(2)
    policy_multiply(0)
    policy_relay(1)
    anchor_multiply(3)
    policy_spread(3)
    policy_multiply(1)
    policy_relay(2)
    policy_relay(3)
    policy_multiply(2)
    compute_near(plane(3))
    relayed(8)
    compute_last(plane(3))

    everyone = [
        (t, dy, dx, dc) for t in (3, 2, 1, 0) for dy, dx, dc in itertools.product((1, 0), repeat=3)
    ][:-1]
    arrivals = []
    for j, (t, dy, dx, dc) in enumerate(everyone):
        there = chip_at(plane(t), dy, dx) * 2 + (core + dc) % 2
        ref = table.at[core, chip]
        copy = remote(ref, ref, m_send.at[j], m_recv.at[me], there)
        copy.start()
        sends.append(copy)
        arrivals.append(remote(ref, ref, m_send.at[j], m_recv.at[there], there))
    for copy in waits:
        copy.wait()
    for copy in sends:
        copy.wait_send()
    for copy in arrivals:
        copy.wait_recv()
    margin_out[...] = table[...]


def finish_kernel(
    gradient,
    policy,
    anchor,
    moment,
    second,
    table,
    pair_index,
    noisy_flags,
    policy_out,
    anchor_out,
    moment_out,
    second_out,
    loss_out,
):
    updated = adam_update(gradient[...], policy[...], anchor[...], moment[...], second[...])
    for out, value in zip((policy_out, anchor_out, moment_out, second_out), updated):
        out[...] = value
    margins = table[0] + table[1]
    sequence = lax.broadcasted_iota(jnp.int32, margins.shape, 0)

    def margin_of(index):
        return jnp.sum(jnp.where(sequence == index, margins, 0.0), axis=0, keepdims=True)

    for p in range(noisy_flags.shape[0]):
        gap = margin_of(pair_index[p, 0]) - margin_of(pair_index[p, 1])
        gap = jnp.where(noisy_flags[p] == 1, -gap, gap)
        tail = jnp.log(1.0 + jnp.exp(-jnp.abs(gap)))
        loss = (1.0 - smoothing) * (tail - jnp.minimum(gap, 0.0)) + smoothing * (
            tail + jnp.maximum(gap, 0.0)
        )
        loss_out[p] = loss[0, 0]


def fused_shards(n, tokens, cotangent, policy, anchor, moment, second, readout, pair_index, noisy_flags):
    tokens_own, depth = tokens.shape
    rows, channels = policy.shape
    half = channels // 2
    block = 2 * rows
    low = half // 2
    seq_chip = 2 * tokens_own // LEN
    sizes = (n, rows, tokens_own, half)
    bf, f32 = jnp.bfloat16, jnp.float32
    vmem, dma = pltpu.VMEM, pltpu.SemaphoreType.DMA
    hbm = pl.BlockSpec(memory_space=pl.ANY)
    whole = pl.BlockSpec(memory_space=pltpu.VMEM)
    weight = jax.ShapeDtypeStruct((rows, channels), f32)
    gradient, table = pl.pallas_call(
        functools.partial(fused_kernel, sizes),
        out_shape=(weight, jax.ShapeDtypeStruct((2, n // 2, seq_chip, 128), f32)),
        in_specs=[hbm] * 6 + [whole],
        out_specs=(hbm, whole),
        scratch_shapes=[
            vmem((2, tokens_own, depth), bf),
            vmem((2, tokens_own, half), bf),
            vmem((half, 2 * tokens_own), bf),
            vmem((2, rows, half), f32),
            vmem((rows, half), bf),
            vmem((3, 2, rows, half), f32),
            vmem((4, 2, low, block), bf),
            vmem((4, 2, low, block), bf),
            vmem((4, 2, low, block), f32),
            vmem((4, 2, low, block), bf),
            vmem((4, 2, low, block), bf),
            vmem((4, 2, low, block), f32),
            vmem((4, low, block), bf),
            vmem((4, low, block), bf),
            vmem((4, low, block), bf),
            vmem((4, low, block), bf),
            vmem((3, half, block), bf),
            vmem((4, half, block), bf),
            vmem((half, block), f32),
            vmem((2, rows, half), f32),
            vmem((2, depth, half), bf),
            vmem((2, 2, tokens_own, half), f32),
            vmem((2, n // 2, seq_chip, 128), f32),
            dma((16,)),
            dma((16,)),
            dma((16,)),
            dma((4, 4)),
            dma((4, 4)),
            dma((3,)),
            dma((4,)),
            dma((1,)),
            dma((1,)),
            dma((9, 4)),
            dma((9, 4)),
            dma((6, 3)),
            dma((6, 4)),
            dma((n,)),
            dma((n,)),
        ],
        compiler_params=pltpu.CompilerParams(
            collective_id=0, has_side_effects=True, vmem_limit_bytes=56 * 1024 * 1024
        ),
    )(
        tokens,
        cotangent,
        policy,
        anchor,
        moment,
        second,
        readout.reshape(2, 1, half),
    )
    smem = pl.BlockSpec(memory_space=pltpu.SMEM)
    policy_next, anchor_next, moment_next, second_next, pair_loss = pl.pallas_call(
        finish_kernel,
        out_shape=(weight,) * 4 + (jax.ShapeDtypeStruct(noisy_flags.shape, f32),),
        in_specs=[whole] * 6 + [smem] * 2,
        out_specs=(whole,) * 4 + (smem,),
    )(
        gradient,
        policy,
        anchor,
        moment,
        second,
        table.reshape(2, n // 2 * seq_chip, 128),
        pair_index,
        noisy_flags,
    )
    return (policy_next, anchor_next, moment_next, second_next, pair_loss)


def solution(mesh):
    placed = (
        P(("rep", "fsdp"), None),
        P(("rep", "fsdp"), None),
        P("fsdp", None),
        P("fsdp", None),
        P("fsdp", None),
        P("fsdp", None),
        P(),
        P(("rep", "fsdp"), None),
        P(("rep", "fsdp")),
    )
    n = mesh.shape["fsdp"]
    body = shards
    if mesh.shape["rep"] == 1 and n == 8 * PLANES:
        body = functools.partial(fused_shards, n)
    return jax.shard_map(
        body,
        mesh=mesh,
        in_specs=placed,
        out_specs=(
            P("fsdp", None),
            P("fsdp", None),
            P("fsdp", None),
            P("fsdp", None),
            P(("rep", "fsdp")),
        ),
        check_vma=False,
    )
```

time: 87.7 us -> 77.7 us (0.89)
  Pallas kernels: 86.9 us -> 76.9 us
    pallas_call x1, Pallas kernels: 84.2 us -> 74.2 us  [fused_shards(): pl.pallas_call(functools.partial(fused_kernel, sizes), out_shape=(weight,...]
where the time goes in v1:
time: 77.7 us; the launch traced here: 77.5 us
  Pallas kernels  76.9 us (99%)
    pallas_call x1, Pallas kernels, fused_shards(): pl.pallas_call(functools.partial(fused_kernel, sizes), out_shape=(weight,...  74.2 us
    pallas_call x1, Pallas kernels, fused_shards(): pl.pallas_call(finish_kernel, out_shape=(weight,) * 4 + (jax.ShapeDtypeSt...  2.67 us

profile of v1, /device:TPU:0, one launch (start us, length us, event | category | flops | bytes accessed | tf_op | source)
XLA Modules:
  0.0 77.5 jit_solution(14980219700305532902)
XLA Ops:
  0.6 74.2 %shard_map.128 = (f32[128,512]{1,0:T(8,128)}, f32[2,16,8,128]{3,2,1,0:T(8,128)}) custom-call(bf16[768,4096]{1,0:T(8,128)(2,1)} %tokens.1, bf16[768,512]{1,0:T(8,128)(2,1)} %cotangent.1, f32[128,512]{1,0:T(8,128)} %policy.3, f32[128,512]{1,0:T(8,128)} %anchor.3, f32[128,512]{1,0:T(8,128)} %moment.3, f32[128,512]{1,0:T(8,128)} %second.3, f32[2,1,256]{2,1,0:T(1,128)} %bitcast.3), custom_call_target="tpu_custom_call" | custom-call | tf_op jit(solution)/shard_map/pallas_call | solution.py:621
  74.9 2.7 %shard_map.129 = (f32[128,512]{1,0:T(8,128)}, f32[128,512]{1,0:T(8,128)}, f32[128,512]{1,0:T(8,128)}, f32[128,512]{1,0:T(8,128)}, f32[2]{0:T(128)}) custom-call(f32[128,512]{1,0:T(8,128)} %get-tuple-element.7.gradient, f32[128,512]{1,0:T(8,128)} %policy.3, f32[128,512]{1,0:T(8,128)} %anchor.3, f32[128,512]{1,0:T(8,128)} %moment.3, f32[128,512]{1,0:T(8,128)} %second.3, ...), custom_call_target="tpu_custom_call" | custom-call | tf_op jit(solution)/shard_map/pallas_call | solution.py:679

commit v2 on v1

--- a/solution.py
+++ b/solution.py
@@ -142,6 +142,7 @@
     xy_recv,
     z_send,
     z_recv,
+    p_send,
     m_send,
     m_recv,
 ):
@@ -216,22 +217,22 @@
         copy.start()
         par_local.append(copy)
 
+    pl.semaphore_wait(barrier, len(others))
+
+    sends = []
+    cot_swap = remote(cotangent.at[:, theirs], cot.at[core], swap_send.at[1], swap_recv.at[1], mate)
+    cot_swap.start()
+    sends.append(cot_swap)
     own_rows = pl.ds(pl.multiple_of(home + core * rows, rows), rows)
     anc_local[0].wait()
     weights[1, own_rows, :] = anc[0].astype(jnp.bfloat16)
-    anc_local[1].wait()
-    anc_send[...] = anc[1].astype(jnp.bfloat16)
-
-    pl.semaphore_wait(barrier, len(others))
-
-    sends = []
 
     def chip_at(zz, dy, dx):
         return zz * 4 + ((py + dy) % 2) * 2 + (px + dx) % 2
 
     kinds = {
         "c": (1, core * (block - EARLY), EARLY),
-        "b": (1, (1 - core) * EARLY, block - EARLY),
+        "a": (1, (1 - core) * EARLY, block - EARLY),
         "p": (0, 0, block),
     }
 
@@ -277,15 +278,51 @@
         ref = part(kind, chip_at(plane(t), dy, dx))
         remote(ref, ref, z_send.at[q, t - 1], z_recv.at[q, plane(t)], z_mate(t)).wait_recv()
 
-    spread("c", 0, pz)
-    z_out("c", 0, chip)
+    middle = jnp.logical_and(pz > 0, pz < PLANES - 1)
+
+    def chain_copies(t):
+        zz = plane(t)
+        ref = part("p", chip_at(zz, 0, 0))
+        up = remote(ref, ref, p_send.at[0, t], z_recv.at[1, zz], (me + 8) % n)
+        down = remote(ref, ref, p_send.at[1, t], z_recv.at[1, zz], (me + n - 8) % n)
+        return zz, up, down
+
+    def far_copy():
+        ref = part("p", chip)
+        return remote(ref, ref, p_send.at[2, 0], z_recv.at[1, pz], z_mate(3))
+
+    def chain_each(t, copies, act):
+        zz, up, down = copies
+        if t < PLANES - 1:
+
+            @pl.when(jnp.logical_and(zz <= pz, pz < PLANES - 1))
+            def _():
+                act(up)
+
+            @pl.when(jnp.logical_and(zz >= pz, pz > 0))
+            def _():
+                act(down)
+
+        if t == 0:
+
+            @pl.when(jnp.logical_not(middle))
+            def _():
+                act(far_copy())
+
+    def chain_step(t):
+        copies = chain_copies(t)
+        if t > 0:
+            copies[1].wait_recv()
+        chain_each(t, copies, lambda copy: copy.start())
+
+    spread("c", 8, pz)
+    z_out("c", 2, chip)
+    anc_local[1].wait()
+    anc_send[...] = anc[1].astype(jnp.bfloat16)
     launch(
         "anc",
         remote(anc_send, weights.at[1, own_rows, :], swap_send.at[0], swap_recv.at[0], mate),
     )
-    cot_swap = remote(cotangent.at[:, theirs], cot.at[core], swap_send.at[1], swap_recv.at[1], mate)
-    cot_swap.start()
-    sends.append(cot_swap)
     tok_swap = {}
     for j, key in enumerate(pieces):
         where = columns(*key)
@@ -308,8 +345,8 @@
         sends.append(copy)
 
     flights["anc"].wait_recv()
-    z_out("b", 4, chip)
-    spread("b", 1, pz)
+    z_out("a", 0, chip)
+    spread("a", 0, pz)
 
     cot_local.wait()
     cot_swap.wait_recv()
@@ -354,14 +391,12 @@
     def send_a(i):
         hop("a1", i, 0, send_a1.at[i], recv_a1.at[i], x_mate)
 
-    def stage_one(i, hold=False, between=None):
+    def stage_one(i, hold=False):
         first((i, 1))
         block_gradient(i, 1, 1)
         block_gradient(i, 1, 0)
         if not hold:
             send_b(i)
-        if between is not None:
-            between()
         first((i, 0))
         block_gradient(i, 0, 1)
         if not hold:
@@ -393,37 +428,35 @@
             copy.start()
             sends.append(copy)
 
-    def early_out():
-        relay("c", 0, pz)
-        z_out("c", 1, chip_at(pz, 0, 1))
-        z_out("c", 2, chip_at(pz, 1, 0))
-
-    def blend_spread(t):
-        z_in("b", 4, t)
-        spread("b", 1 + t, plane(t))
-
-    def blend_relay(t):
-        relay("b", 1 + t, plane(t))
-
-    stage_one(0, between=early_out)
+    def anchor_spread(t):
+        z_in("a", 0, t)
+        spread("a", t, plane(t))
+
+    def anchor_relay(t):
+        relay("a", t, plane(t))
+
+    stage_one(0)
     stage_one(1)
-    blend_relay(0)
-    stage_one(2)
+    stage_one(2, hold=True)
+    relay("c", 8, pz)
+    z_out("c", 3, chip_at(pz, 0, 1))
     stage_two(0)
+    send_b(2)
+    send_a(2)
+    stage_one(3, hold=True)
     stage_two(1)
-    stage_one(3, hold=True)
+    stage_three(0)
     stage_two(2)
     send_b(3)
     send_a(3)
-    stage_three(0)
     stage_three(1)
-    blend_spread(1)
+    anchor_relay(0)
+    anchor_spread(1)
     stage_three(2)
-    relayed(0)
-    z_out("c", 3, chip_at(pz, 1, 1))
+    z_out("c", 4, chip_at(pz, 1, 0))
     stage_two(3)
-    blend_relay(1)
-    blend_spread(2)
+    anchor_spread(2)
+    anchor_relay(1)
     for a in range(3):
         par_local[a].wait()
         par_swap[a].wait_recv()
@@ -444,8 +477,8 @@
         weights[0, pl.ds(pl.multiple_of(home + r * rows, rows), rows), :] = updated.astype(
             jnp.bfloat16
         )
-    z_out("p", 5, chip)
-    spread("p", 5, pz)
+    chain_step(0)
+    spread("p", 4, pz)
 
     tile = tokens_own
     scale = readout[core]
@@ -469,22 +502,21 @@
             acc[m, i] = value if t == 0 else acc[m, i] + value
 
     def anchor_multiply(t):
-        relayed(1 + t)
+        relayed(t)
         if t > 0:
             for j, (dy, dx) in enumerate(((0, 0), (0, 1), (1, 0), (1, 1))):
-                z_in("c", j, t, dy, dx)
+                z_in("c", 2 + j, t, dy, dx)
         multiply(1, t)
 
     def policy_multiply(t):
-        relayed(5 + t)
+        relayed(4 + t)
         multiply(0, t)
 
     def policy_spread(t):
-        z_in("p", 5, t)
-        spread("p", 5 + t, plane(t))
+        spread("p", 4 + t, plane(t))
 
     def policy_relay(t):
-        relay("p", 5 + t, plane(t))
+        relay("p", 4 + t, plane(t))
 
     def spot(zz, dy, dx):
         return pl.ds(pl.multiple_of(chip_at(zz, dy, dx) * block, block), block)
@@ -530,44 +562,63 @@
     copy.start()
     waits.append(copy)
 
-    blend_relay(2)
-    blend_spread(3)
+    anchor_spread(3)
+    relayed(8)
     anchor_multiply(0)
+    anchor_relay(2)
+    policy_relay(0)
+    chain_step(1)
+
+    @pl.when(middle)
+    def _():
+        chain_step(2)
+
+    policy_spread(1)
+    z_out("c", 5, chip_at(pz, 1, 1))
+    anchor_relay(3)
+    policy_multiply(0)
+
+    @pl.when(jnp.logical_not(middle))
+    def _():
+        chain_step(2)
+
+    chain_step(3)
+    policy_spread(2)
+    policy_relay(1)
+    policy_spread(3)
     anchor_multiply(1)
-    policy_relay(0)
-    policy_spread(1)
-    blend_relay(3)
     anchor_multiply(2)
-    policy_spread(2)
-    policy_multiply(0)
-    policy_relay(1)
+    policy_relay(2)
     anchor_multiply(3)
-    policy_spread(3)
     policy_multiply(1)
-    policy_relay(2)
     policy_relay(3)
+    compute_near(plane(3))
     policy_multiply(2)
-    compute_near(plane(3))
-    relayed(8)
+    for copy in waits:
+        copy.wait()
+    for copy in sends:
+        copy.wait_send()
+    for t in range(PLANES):
+        chain_each(t, chain_copies(t), lambda copy: copy.wait_send())
+    relayed(7)
     compute_last(plane(3))
 
     everyone = [
         (t, dy, dx, dc) for t in (3, 2, 1, 0) for dy, dx, dc in itertools.product((1, 0), repeat=3)
     ][:-1]
+    sent = []
     arrivals = []
     for j, (t, dy, dx, dc) in enumerate(everyone):
         there = chip_at(plane(t), dy, dx) * 2 + (core + dc) % 2
         ref = table.at[core, chip]
         copy = remote(ref, ref, m_send.at[j], m_recv.at[me], there)
         copy.start()
-        sends.append(copy)
+        sent.append(copy)
         arrivals.append(remote(ref, ref, m_send.at[j], m_recv.at[there], there))
-    for copy in waits:
-        copy.wait()
-    for copy in sends:
-        copy.wait_send()
     for copy in arrivals:
         copy.wait_recv()
+    for copy in sent:
+        copy.wait_send()
     margin_out[...] = table[...]
 
 
@@ -660,6 +711,7 @@
             dma((9, 4)),
             dma((6, 3)),
             dma((6, 4)),
+            dma((3, 4)),
             dma((n,)),
             dma((n,)),
         ],

time: 77.7 us -> 72.8 us (0.937)
  Pallas kernels: 76.9 us -> 71.9 us
    pallas_call x1, Pallas kernels: 74.2 us -> 69.3 us  [fused_shards(): pl.pallas_call(functools.partial(fused_kernel, sizes), out_shape=(weight,...]
where the time goes in v2:
time: 72.8 us; the launch traced here: 72.6 us
  Pallas kernels  71.9 us (99%)
    pallas_call x1, Pallas kernels, fused_shards(): pl.pallas_call(functools.partial(fused_kernel, sizes), out_shape=(weight,...  69.3 us
    pallas_call x1, Pallas kernels, fused_shards(): pl.pallas_call(finish_kernel, out_shape=(weight,) * 4 + (jax.ShapeDtypeSt...  2.67 us

profile of v2, /device:TPU:0, one launch (start us, length us, event | category | flops | bytes accessed | tf_op | source)
XLA Modules:
  0.0 72.6 jit_solution(11536573561542182144)
XLA Ops:
  0.6 69.3 %shard_map.128 = (f32[128,512]{1,0:T(8,128)}, f32[2,16,8,128]{3,2,1,0:T(8,128)}) custom-call(bf16[768,4096]{1,0:T(8,128)(2,1)} %tokens.1, bf16[768,512]{1,0:T(8,128)(2,1)} %cotangent.1, f32[128,512]{1,0:T(8,128)} %policy.3, f32[128,512]{1,0:T(8,128)} %anchor.3, f32[128,512]{1,0:T(8,128)} %moment.3, f32[128,512]{1,0:T(8,128)} %second.3, f32[2,1,256]{2,1,0:T(1,128)} %bitcast.3), custom_call_target="tpu_custom_call" | custom-call | tf_op jit(solution)/shard_map/pallas_call | solution.py:672
  69.9 2.7 %shard_map.129 = (f32[128,512]{1,0:T(8,128)}, f32[128,512]{1,0:T(8,128)}, f32[128,512]{1,0:T(8,128)}, f32[128,512]{1,0:T(8,128)}, f32[2]{0:T(128)}) custom-call(f32[128,512]{1,0:T(8,128)} %get-tuple-element.7.gradient, f32[128,512]{1,0:T(8,128)} %policy.3, f32[128,512]{1,0:T(8,128)} %anchor.3, f32[128,512]{1,0:T(8,128)} %moment.3, f32[128,512]{1,0:T(8,128)} %second.3, ...), custom_call_target="tpu_custom_call" | custom-call | tf_op jit(solution)/shard_map/pallas_call | solution.py:731

commit v3 on v2

--- a/solution.py
+++ b/solution.py
@@ -104,8 +104,10 @@
     moment,
     second,
     readout,
+    pair_index,
+    noisy_flags,
     gradient_out,
-    margin_out,
+    loss_out,
     tok,
     cot,
     cot_t,
@@ -129,22 +131,14 @@
     weights,
     acc,
     table,
-    local_sem,
-    swap_send,
-    swap_recv,
-    rs_send,
+    own_sem,
+    tok_sem,
+    anc_sem,
     rs_recv,
-    rz_send,
-    rz_recv,
-    out_send,
-    out_recv,
-    xy_send,
     xy_recv,
-    z_send,
     z_recv,
-    p_send,
-    m_send,
-    m_recv,
+    out_sem,
+    sent_sem,
 ):
     n, rows, tokens_own, half = sizes
     block = 2 * rows
@@ -164,6 +158,7 @@
 
     top = pz // 2
     near = pz + top * (3 - 2 * pz)
+    middle = jnp.logical_and(pz > 0, pz < PLANES - 1)
 
     def plane(t):
         there = (near, 1 - near, 2, 3)[t]
@@ -182,6 +177,9 @@
             device_id_type=MESH_ID,
         )
 
+    def await_bytes(ref, sem):
+        pltpu.make_async_copy(ref, ref, sem).wait()
+
     barrier = pltpu.get_barrier_semaphore()
     others = [mate, x_mate, y_mate] + [z_mate(t) for t in (1, 2, 3)]
     for other in others:
@@ -197,34 +195,35 @@
 
     pieces = [(i, dy) for i in range(PLANES) for dy in (1, 0)]
 
-    anc_local = []
     for r, side in enumerate((mine, theirs)):
-        copy = pltpu.make_async_copy(anchor.at[:, side], anc.at[r], local_sem.at[r])
-        copy.start()
-        anc_local.append(copy)
-    cot_local = pltpu.make_async_copy(cotangent.at[:, mine], cot.at[core], local_sem.at[2])
-    cot_local.start()
-    tok_local = {}
-    for j, key in enumerate(pieces):
-        where = columns(*key)
-        tok_local[key] = pltpu.make_async_copy(
-            tokens.at[:, where], tok.at[core, :, where], local_sem.at[8 + j]
-        )
-        tok_local[key].start()
-    par_local = []
-    for a in range(3):
-        copy = pltpu.make_async_copy(params[a].at[:, mine], par.at[a, core], local_sem.at[3 + a])
-        copy.start()
-        par_local.append(copy)
-
+        pltpu.make_async_copy(anchor.at[:, side], anc.at[r], anc_sem.at[r]).start()
+    pltpu.make_async_copy(cotangent.at[:, mine], cot.at[core], own_sem.at[0]).start()
+
+    def load(j):
+        where = columns(*pieces[j])
+        pltpu.make_async_copy(
+            tokens.at[:, where], tok.at[core, :, where], tok_sem.at[j]
+        ).start()
+
+    load(0)
+    load(1)
     pl.semaphore_wait(barrier, len(others))
 
-    sends = []
-    cot_swap = remote(cotangent.at[:, theirs], cot.at[core], swap_send.at[1], swap_recv.at[1], mate)
-    cot_swap.start()
-    sends.append(cot_swap)
+    unit = half * 2
+    sent = {}
+
+    def launch(group, src, dst, recv_sem, device):
+        remote(src, dst, sent_sem.at[group], recv_sem, device).start()
+        count = 1
+        for extent in src.shape:
+            count *= extent
+        sent[group] = sent.get(group, 0) + count * jnp.dtype(src.dtype).itemsize // unit
+
+    SWAP, REDUCE, SPREAD, POLICY, CHAIN, MARGIN, TOKENS = range(7)
+
+    launch(SWAP, cotangent.at[:, theirs], cot.at[core], own_sem.at[0], mate)
     own_rows = pl.ds(pl.multiple_of(home + core * rows, rows), rows)
-    anc_local[0].wait()
+    await_bytes(anc.at[0], anc_sem.at[0])
     weights[1, own_rows, :] = anc[0].astype(jnp.bfloat16)
 
     def chip_at(zz, dy, dx):
@@ -243,121 +242,78 @@
             start = start + which * count
         return weights.at[m, pl.ds(pl.multiple_of(k * block + start, 16), count), :]
 
-    flights = {}
-
-    def launch(name, copy):
-        copy.start()
-        flights[name] = copy
-        sends.append(copy)
+    def some_rows(count, m=0):
+        return weights.at[m, pl.ds(0, count), :]
 
     def spread(kind, q, zz):
         ref = part(kind, chip_at(zz, 0, 0))
-        launch((q, 0), remote(ref, ref, xy_send.at[q, 0], xy_recv.at[q, 0], x_mate))
-        launch((q, 1), remote(ref, ref, xy_send.at[q, 1], xy_recv.at[q, 1], y_mate))
+        group = POLICY if kind == "p" else SPREAD
+        launch(group, ref, ref, xy_recv.at[q, 0], x_mate)
+        launch(group, ref, ref, xy_recv.at[q, 0], y_mate)
 
     def relay(kind, q, zz):
-        flights[q, 1].wait_recv()
+        await_bytes(some_rows(2 * kinds[kind][2]), xy_recv.at[q, 0])
+        group = POLICY if kind == "p" else SPREAD
         ref = part(kind, chip_at(zz, 1, 0), 0)
-        launch((q, 2), remote(ref, ref, xy_send.at[q, 2], xy_recv.at[q, 2], x_mate))
-        flights[q, 0].wait_recv()
+        launch(group, ref, ref, xy_recv.at[q, 1], x_mate)
         ref = part(kind, chip_at(zz, 0, 1), 1)
-        launch((q, 3), remote(ref, ref, xy_send.at[q, 3], xy_recv.at[q, 3], y_mate))
-
-    def relayed(q):
-        flights[q, 2].wait_recv()
-        flights[q, 3].wait_recv()
+        launch(group, ref, ref, xy_recv.at[q, 1], y_mate)
+
+    def relayed(kind, q):
+        await_bytes(some_rows(kinds[kind][2]), xy_recv.at[q, 1])
 
     def z_out(kind, q, k):
         for t in (1, 2, 3):
             ref = part(kind, k)
-            copy = remote(ref, ref, z_send.at[q, t - 1], z_recv.at[q, pz], z_mate(t))
-            copy.start()
-            sends.append(copy)
-
-    def z_in(kind, q, t, dy=0, dx=0):
-        ref = part(kind, chip_at(plane(t), dy, dx))
-        remote(ref, ref, z_send.at[q, t - 1], z_recv.at[q, plane(t)], z_mate(t)).wait_recv()
-
-    middle = jnp.logical_and(pz > 0, pz < PLANES - 1)
-
-    def chain_copies(t):
+            launch(SPREAD, ref, ref, z_recv.at[q, pz], z_mate(t))
+
+    def z_in(q, t, count):
+        await_bytes(some_rows(count), z_recv.at[q, plane(t)])
+
+    def chain_each(t, act):
         zz = plane(t)
         ref = part("p", chip_at(zz, 0, 0))
-        up = remote(ref, ref, p_send.at[0, t], z_recv.at[1, zz], (me + 8) % n)
-        down = remote(ref, ref, p_send.at[1, t], z_recv.at[1, zz], (me + n - 8) % n)
-        return zz, up, down
-
-    def far_copy():
-        ref = part("p", chip)
-        return remote(ref, ref, p_send.at[2, 0], z_recv.at[1, pz], z_mate(3))
-
-    def chain_each(t, copies, act):
-        zz, up, down = copies
+
+        def to(device):
+            act(remote(ref, ref, sent_sem.at[CHAIN], z_recv.at[2, zz], device))
+
         if t < PLANES - 1:
-
-            @pl.when(jnp.logical_and(zz <= pz, pz < PLANES - 1))
-            def _():
-                act(up)
-
-            @pl.when(jnp.logical_and(zz >= pz, pz > 0))
-            def _():
-                act(down)
-
+            pl.when(jnp.logical_and(zz <= pz, pz < PLANES - 1))(lambda: to((me + 8) % n))
+            pl.when(jnp.logical_and(zz >= pz, pz > 0))(lambda: to((me + n - 8) % n))
         if t == 0:
-
-            @pl.when(jnp.logical_not(middle))
-            def _():
-                act(far_copy())
+            pl.when(jnp.logical_not(middle))(lambda: to(z_mate(3)))
 
     def chain_step(t):
-        copies = chain_copies(t)
         if t > 0:
-            copies[1].wait_recv()
-        chain_each(t, copies, lambda copy: copy.start())
+            z_in(2, t, block)
+        chain_each(t, lambda copy: copy.start())
 
     spread("c", 8, pz)
-    z_out("c", 2, chip)
-    anc_local[1].wait()
+    z_out("c", 0, chip)
+    await_bytes(anc.at[1], anc_sem.at[1])
     anc_send[...] = anc[1].astype(jnp.bfloat16)
-    launch(
-        "anc",
-        remote(anc_send, weights.at[1, own_rows, :], swap_send.at[0], swap_recv.at[0], mate),
-    )
-    tok_swap = {}
+    launch(SWAP, anc_send, weights.at[1, own_rows, :], anc_sem.at[2], mate)
+    for j in range(2, len(pieces)):
+        load(j)
     for j, key in enumerate(pieces):
         where = columns(*key)
-        tok_swap[key] = remote(
-            tokens.at[:, where],
-            tok.at[core, :, where],
-            swap_send.at[8 + j],
-            swap_recv.at[8 + j],
-            mate,
-        )
-        tok_swap[key].start()
-        sends.append(tok_swap[key])
-    par_swap = []
+        launch(TOKENS, tokens.at[:, where], tok.at[core, :, where], tok_sem.at[j], mate)
     for a in range(3):
-        copy = remote(
-            params[a].at[:, theirs], par.at[a, core], swap_send.at[2 + a], swap_recv.at[2 + a], mate
-        )
-        copy.start()
-        par_swap.append(copy)
-        sends.append(copy)
-
-    flights["anc"].wait_recv()
-    z_out("a", 0, chip)
+        pltpu.make_async_copy(params[a].at[:, mine], par.at[a, core], own_sem.at[1]).start()
+        launch(SWAP, params[a].at[:, theirs], par.at[a, core], own_sem.at[1], mate)
+
+    await_bytes(anc_send, anc_sem.at[2])
+    z_out("a", 1, chip)
     spread("a", 0, pz)
 
-    cot_local.wait()
-    cot_swap.wait_recv()
+    await_bytes(cot, own_sem.at[0])
     for r in range(2):
         cot_t[:, r * tokens_own : (r + 1) * tokens_own] = (
             cot[r].astype(jnp.float32).T.astype(jnp.bfloat16)
         )
 
     def first(key):
-        tok_local[key].wait()
-        tok_swap[key].wait_recv()
+        await_bytes(tok.at[:, :, columns(*key)], tok_sem.at[pieces.index(key)])
 
     def block_gradient(i, dy, dx):
         target = chip_at(plane(3 - i), dy, dx)
@@ -377,19 +333,11 @@
         else:
             keep_b[i, dx] = total[low:]
 
-    hops = {}
-
-    def hop(name, i, slot, src, dst, device):
-        copy = remote(src, dst, rs_send.at[slot, i], rs_recv.at[slot, i], device)
-        copy.start()
-        hops[name, i] = copy
-        sends.append(copy)
-
     def send_b(i):
-        hop("b1", i, 1, send_b1.at[i], recv_b1.at[i], y_mate)
+        launch(REDUCE, send_b1.at[i], recv_b1.at[i], rs_recv.at[1, i], y_mate)
 
     def send_a(i):
-        hop("a1", i, 0, send_a1.at[i], recv_a1.at[i], x_mate)
+        launch(REDUCE, send_a1.at[i], recv_a1.at[i], rs_recv.at[0, i], x_mate)
 
     def stage_one(i, hold=False):
         first((i, 1))
@@ -404,17 +352,17 @@
         block_gradient(i, 0, 0)
 
     def stage_two(i):
-        hops["a1", i].wait_recv()
+        await_bytes(recv_a1.at[i], rs_recv.at[0, i])
         send_a2[i] = (keep_a[i, 1] + recv_a1[i, 1].astype(jnp.float32)).astype(jnp.bfloat16)
-        hop("a2", i, 2, send_a2.at[i], recv_a2.at[i], y_mate)
-        hops["b1", i].wait_recv()
+        launch(REDUCE, send_a2.at[i], recv_a2.at[i], rs_recv.at[2, i], y_mate)
+        await_bytes(recv_b1.at[i], rs_recv.at[1, i])
         send_b2[i] = (keep_b[i, 1] + recv_b1[i, 1].astype(jnp.float32)).astype(jnp.bfloat16)
-        hop("b2", i, 3, send_b2.at[i], recv_b2.at[i], x_mate)
+        launch(REDUCE, send_b2.at[i], recv_b2.at[i], rs_recv.at[3, i], x_mate)
 
     def stage_three(i):
-        hops["a2", i].wait_recv()
+        await_bytes(recv_a2.at[i], rs_recv.at[2, i])
         total_a = keep_a[i, 0] + recv_a1[i, 0].astype(jnp.float32) + recv_a2[i].astype(jnp.float32)
-        hops["b2", i].wait_recv()
+        await_bytes(recv_b2.at[i], rs_recv.at[3, i])
         total_b = keep_b[i, 0] + recv_b1[i, 0].astype(jnp.float32) + recv_b2[i].astype(jnp.float32)
         if i == PLANES - 1:
             grad_own[:low] = total_a
@@ -422,14 +370,10 @@
         else:
             send_z[i, :low] = total_a.astype(jnp.bfloat16)
             send_z[i, low:] = total_b.astype(jnp.bfloat16)
-            copy = remote(
-                send_z.at[i], recv_z.at[pz], rz_send.at[i], rz_recv.at[pz], z_mate(3 - i)
-            )
-            copy.start()
-            sends.append(copy)
+            launch(REDUCE, send_z.at[i], recv_z.at[pz], rs_recv.at[4, 0], z_mate(3 - i))
 
     def anchor_spread(t):
-        z_in("a", 0, t)
+        z_in(1, t, block - EARLY)
         spread("a", t, plane(t))
 
     def anchor_relay(t):
@@ -439,32 +383,26 @@
     stage_one(1)
     stage_one(2, hold=True)
     relay("c", 8, pz)
-    z_out("c", 3, chip_at(pz, 0, 1))
+    z_out("c", 0, chip_at(pz, 0, 1))
     stage_two(0)
     send_b(2)
     send_a(2)
     stage_one(3, hold=True)
     stage_two(1)
     stage_three(0)
+    anchor_relay(0)
     stage_two(2)
     send_b(3)
     send_a(3)
     stage_three(1)
-    anchor_relay(0)
     anchor_spread(1)
     stage_three(2)
-    z_out("c", 4, chip_at(pz, 1, 0))
+    z_out("c", 0, chip_at(pz, 1, 0))
     stage_two(3)
     anchor_spread(2)
     anchor_relay(1)
-    for a in range(3):
-        par_local[a].wait()
-        par_swap[a].wait_recv()
-    for t in (3, 2, 1):
-        zz = plane(t)
-        remote(
-            send_z.at[0], recv_z.at[zz], rz_send.at[0], rz_recv.at[zz], z_mate(t)
-        ).wait_recv()
+    await_bytes(par, own_sem.at[1])
+    await_bytes(recv_z.at[pl.ds(0, PLANES - 1)], rs_recv.at[4, 0])
     stage_three(3)
     gradient = grad_own[...]
     for t in (1, 2, 3):
@@ -502,14 +440,13 @@
             acc[m, i] = value if t == 0 else acc[m, i] + value
 
     def anchor_multiply(t):
-        relayed(t)
+        relayed("a", t)
         if t > 0:
-            for j, (dy, dx) in enumerate(((0, 0), (0, 1), (1, 0), (1, 1))):
-                z_in("c", 2 + j, t, dy, dx)
+            z_in(0, t, 4 * EARLY)
         multiply(1, t)
 
     def policy_multiply(t):
-        relayed(4 + t)
+        relayed("p", 4 + t)
         multiply(0, t)
 
     def policy_spread(t):
@@ -548,22 +485,15 @@
                 )
                 gap = jnp.sum(gap, axis=0, keepdims=True)
                 gap = jnp.sum(gap, axis=1, keepdims=True)
-                table[core, chip, pl.ds(i * (tile // LEN) + j, 1), :] = jnp.broadcast_to(
+                table[me, pl.ds(i * (tile // LEN) + j, 1), :] = jnp.broadcast_to(
                     gap * (1.0 / LEN), (1, 128)
                 )
 
-    waits = []
-    copy = pltpu.make_async_copy(result.at[core], gradient_out.at[:, mine], local_sem.at[6])
-    copy.start()
-    waits.append(copy)
-    copy = remote(
-        result.at[1 - core], gradient_out.at[:, mine], out_send.at[0], out_recv.at[0], mate
-    )
-    copy.start()
-    waits.append(copy)
+    pltpu.make_async_copy(result.at[core], gradient_out.at[:, mine], out_sem.at[0]).start()
+    launch(REDUCE, result.at[1 - core], gradient_out.at[:, mine], out_sem.at[0], mate)
 
     anchor_spread(3)
-    relayed(8)
+    relayed("c", 8)
     anchor_multiply(0)
     anchor_relay(2)
     policy_relay(0)
@@ -574,7 +504,7 @@
         chain_step(2)
 
     policy_spread(1)
-    z_out("c", 5, chip_at(pz, 1, 1))
+    z_out("c", 0, chip_at(pz, 1, 1))
     anchor_relay(3)
     policy_multiply(0)
 
@@ -594,32 +524,39 @@
     policy_relay(3)
     compute_near(plane(3))
     policy_multiply(2)
-    for copy in waits:
-        copy.wait()
-    for copy in sends:
-        copy.wait_send()
-    for t in range(PLANES):
-        chain_each(t, chain_copies(t), lambda copy: copy.wait_send())
-    relayed(7)
+    await_bytes(gradient_out, out_sem.at[0])
+    await_bytes(tok.at[0], sent_sem.at[TOKENS])
+    for group in (SWAP, REDUCE, SPREAD, POLICY):
+        await_bytes(some_rows(sent[group]), sent_sem.at[group])
+    pl.when(middle)(lambda: await_bytes(some_rows(4 * block), sent_sem.at[CHAIN]))
+    pl.when(jnp.logical_not(middle))(lambda: await_bytes(some_rows(2 * block), sent_sem.at[CHAIN]))
+    relayed("p", 7)
     compute_last(plane(3))
 
     everyone = [
         (t, dy, dx, dc) for t in (3, 2, 1, 0) for dy, dx, dc in itertools.product((1, 0), repeat=3)
     ][:-1]
-    sent = []
-    arrivals = []
-    for j, (t, dy, dx, dc) in enumerate(everyone):
+    for t, dy, dx, dc in everyone:
         there = chip_at(plane(t), dy, dx) * 2 + (core + dc) % 2
-        ref = table.at[core, chip]
-        copy = remote(ref, ref, m_send.at[j], m_recv.at[me], there)
-        copy.start()
-        sent.append(copy)
-        arrivals.append(remote(ref, ref, m_send.at[j], m_recv.at[there], there))
-    for copy in arrivals:
-        copy.wait_recv()
-    for copy in sent:
-        copy.wait_send()
-    margin_out[...] = table[...]
+        ref = table.at[me]
+        remote(ref, ref, sent_sem.at[MARGIN], out_sem.at[1], there).start()
+    await_bytes(table.at[pl.ds(0, n - 1)], out_sem.at[1])
+    await_bytes(table.at[pl.ds(0, n - 1)], sent_sem.at[MARGIN])
+    margins = table[...].reshape(n // 2, 2, -1, 128)
+    margins = (margins[:, 0] + margins[:, 1]).reshape(-1, 128)
+    sequence = lax.broadcasted_iota(jnp.int32, margins.shape, 0)
+
+    def margin_of(index):
+        return jnp.sum(jnp.where(sequence == index, margins, 0.0), axis=0, keepdims=True)
+
+    for p in range(noisy_flags.shape[0]):
+        gap = margin_of(pair_index[p, 0]) - margin_of(pair_index[p, 1])
+        gap = jnp.where(noisy_flags[p] == 1, -gap, gap)
+        tail = jnp.log(1.0 + jnp.exp(-jnp.abs(gap)))
+        loss = (1.0 - smoothing) * (tail - jnp.minimum(gap, 0.0)) + smoothing * (
+            tail + jnp.maximum(gap, 0.0)
+        )
+        loss_out[p] = loss[0, 0]
 
 
 def finish_kernel(
@@ -628,9 +565,7 @@
     anchor,
     moment,
     second,
-    table,
-    pair_index,
-    noisy_flags,
+    loss,
     policy_out,
     anchor_out,
     moment_out,
@@ -640,20 +575,8 @@
     updated = adam_update(gradient[...], policy[...], anchor[...], moment[...], second[...])
     for out, value in zip((policy_out, anchor_out, moment_out, second_out), updated):
         out[...] = value
-    margins = table[0] + table[1]
-    sequence = lax.broadcasted_iota(jnp.int32, margins.shape, 0)
-
-    def margin_of(index):
-        return jnp.sum(jnp.where(sequence == index, margins, 0.0), axis=0, keepdims=True)
-
-    for p in range(noisy_flags.shape[0]):
-        gap = margin_of(pair_index[p, 0]) - margin_of(pair_index[p, 1])
-        gap = jnp.where(noisy_flags[p] == 1, -gap, gap)
-        tail = jnp.log(1.0 + jnp.exp(-jnp.abs(gap)))
-        loss = (1.0 - smoothing) * (tail - jnp.minimum(gap, 0.0)) + smoothing * (
-            tail + jnp.maximum(gap, 0.0)
-        )
-        loss_out[p] = loss[0, 0]
+    for p in range(loss.shape[0]):
+        loss_out[p] = loss[p]
 
 
 def fused_shards(n, tokens, cotangent, policy, anchor, moment, second, readout, pair_index, noisy_flags):
@@ -662,18 +585,19 @@
     half = channels // 2
     block = 2 * rows
     low = half // 2
-    seq_chip = 2 * tokens_own // LEN
     sizes = (n, rows, tokens_own, half)
     bf, f32 = jnp.bfloat16, jnp.float32
     vmem, dma = pltpu.VMEM, pltpu.SemaphoreType.DMA
     hbm = pl.BlockSpec(memory_space=pl.ANY)
     whole = pl.BlockSpec(memory_space=pltpu.VMEM)
+    smem = pl.BlockSpec(memory_space=pltpu.SMEM)
     weight = jax.ShapeDtypeStruct((rows, channels), f32)
-    gradient, table = pl.pallas_call(
+    losses = jax.ShapeDtypeStruct(noisy_flags.shape, f32)
+    gradient, loss = pl.pallas_call(
         functools.partial(fused_kernel, sizes),
-        out_shape=(weight, jax.ShapeDtypeStruct((2, n // 2, seq_chip, 128), f32)),
-        in_specs=[hbm] * 6 + [whole],
-        out_specs=(hbm, whole),
+        out_shape=(weight, losses),
+        in_specs=[hbm] * 6 + [whole] + [smem] * 2,
+        out_specs=(hbm, smem),
         scratch_shapes=[
             vmem((2, tokens_own, depth), bf),
             vmem((2, tokens_own, half), bf),
@@ -697,23 +621,15 @@
             vmem((2, rows, half), f32),
             vmem((2, depth, half), bf),
             vmem((2, 2, tokens_own, half), f32),
-            vmem((2, n // 2, seq_chip, 128), f32),
-            dma((16,)),
-            dma((16,)),
-            dma((16,)),
-            dma((4, 4)),
-            dma((4, 4)),
+            vmem((n, 2 * tokens_own // LEN, 128), f32),
+            dma((2,)),
+            dma((8,)),
             dma((3,)),
-            dma((4,)),
-            dma((1,)),
-            dma((1,)),
-            dma((9, 4)),
-            dma((9, 4)),
-            dma((6, 3)),
-            dma((6, 4)),
+            dma((5, 4)),
+            dma((9, 2)),
             dma((3, 4)),
-            dma((n,)),
-            dma((n,)),
+            dma((2,)),
+            dma((7,)),
         ],
         compiler_params=pltpu.CompilerParams(
             collective_id=0, has_side_effects=True, vmem_limit_bytes=56 * 1024 * 1024
@@ -726,23 +642,15 @@
         moment,
         second,
         readout.reshape(2, 1, half),
-    )
-    smem = pl.BlockSpec(memory_space=pltpu.SMEM)
+        pair_index,
+        noisy_flags,
+    )
     policy_next, anchor_next, moment_next, second_next, pair_loss = pl.pallas_call(
         finish_kernel,
-        out_shape=(weight,) * 4 + (jax.ShapeDtypeStruct(noisy_flags.shape, f32),),
-        in_specs=[whole] * 6 + [smem] * 2,
+        out_shape=(weight,) * 4 + (losses,),
+        in_specs=[whole] * 5 + [smem],
         out_specs=(whole,) * 4 + (smem,),
-    )(
-        gradient,
-        policy,
-        anchor,
-        moment,
-        second,
-        table.reshape(2, n // 2 * seq_chip, 128),
-        pair_index,
-        noisy_flags,
-    )
+    )(gradient, policy, anchor, moment, second, loss)
     return (policy_next, anchor_next, moment_next, second_next, pair_loss)
 
 

time: 72.8 us -> 69.5 us (0.955)
  Pallas kernels: 71.9 us -> 68.7 us
    pallas_call x1, Pallas kernels: 69.3 us -> 66.2 us  [fused_shards(): pl.pallas_call(functools.partial(fused_kernel, sizes), out_shape=(weight,...]
where the time goes in v3:
time: 69.5 us; the launch traced here: 69.3 us
  Pallas kernels  68.7 us (99%)
    pallas_call x1, Pallas kernels, fused_shards(): pl.pallas_call(functools.partial(fused_kernel, sizes), out_shape=(weight,...  66.2 us
    pallas_call x1, Pallas kernels, fused_shards(): pl.pallas_call(finish_kernel, out_shape=(weight,) * 4 + (losses,), in_spe...  2.45 us

profile of v3, /device:TPU:0, one launch (start us, length us, event | category | flops | bytes accessed | tf_op | source)
XLA Modules:
  0.0 69.3 jit_solution(12111825091720305285)
XLA Ops:
  0.6 66.2 %shard_map.128 = (f32[128,512]{1,0:T(8,128)}, f32[2]{0:T(128)}) custom-call(bf16[768,4096]{1,0:T(8,128)(2,1)} %tokens.1, bf16[768,512]{1,0:T(8,128)(2,1)} %cotangent.1, f32[128,512]{1,0:T(8,128)} %policy.3, f32[128,512]{1,0:T(8,128)} %anchor.3, f32[128,512]{1,0:T(8,128)} %moment.3, f32[128,512]{1,0:T(8,128)} %second.3, f32[2,1,256]{2,1,0:T(1,128)} %bitcast.1, ...), custom_call_target="tpu_custom_call" | custom-call | tf_op jit(solution)/shard_map/pallas_call | solution.py:596
  66.9 2.5 %shard_map.129 = (f32[128,512]{1,0:T(8,128)}, f32[128,512]{1,0:T(8,128)}, f32[128,512]{1,0:T(8,128)}, f32[128,512]{1,0:T(8,128)}, f32[2]{0:T(128)}) custom-call(f32[128,512]{1,0:T(8,128)} %get-tuple-element.7.gradient, f32[128,512]{1,0:T(8,128)} %policy.3, f32[128,512]{1,0:T(8,128)} %anchor.3, f32[128,512]{1,0:T(8,128)} %moment.3, f32[128,512]{1,0:T(8,128)} %second.3, ...), custom_call_target="tpu_custom_call" | custom-call | tf_op jit(solution)/shard_map/pallas_call | solution.py:648

commit v4 on v3

--- a/solution.py
+++ b/solution.py
@@ -80,8 +80,8 @@
     return (policy_next, anchor_next, moment_next, second_next, pair_loss)
 
 
+LOG2E = 1.4426950408889634
 PLANES = 4
-EARLY = 64
 MESH_ID = pl.DeviceIdType.MESH
 
 
@@ -223,6 +223,9 @@
 
     launch(SWAP, cotangent.at[:, theirs], cot.at[core], own_sem.at[0], mate)
     own_rows = pl.ds(pl.multiple_of(home + core * rows, rows), rows)
+    await_bytes(anc.at[1], anc_sem.at[1])
+    anc_send[...] = anc[1].astype(jnp.bfloat16)
+    launch(SWAP, anc_send, weights.at[1, own_rows, :], anc_sem.at[2], mate)
     await_bytes(anc.at[0], anc_sem.at[0])
     weights[1, own_rows, :] = anc[0].astype(jnp.bfloat16)
 
@@ -230,8 +233,7 @@
         return zz * 4 + ((py + dy) % 2) * 2 + (px + dx) % 2
 
     kinds = {
-        "c": (1, core * (block - EARLY), EARLY),
-        "a": (1, (1 - core) * EARLY, block - EARLY),
+        "a": (1, 0, block),
         "p": (0, 0, block),
     }
 
@@ -253,6 +255,9 @@
 
     def relay(kind, q, zz):
         await_bytes(some_rows(2 * kinds[kind][2]), xy_recv.at[q, 0])
+        forward(kind, q, zz)
+
+    def forward(kind, q, zz):
         group = POLICY if kind == "p" else SPREAD
         ref = part(kind, chip_at(zz, 1, 0), 0)
         launch(group, ref, ref, xy_recv.at[q, 1], x_mate)
@@ -267,6 +272,11 @@
             ref = part(kind, k)
             launch(SPREAD, ref, ref, z_recv.at[q, pz], z_mate(t))
 
+    def beside(kind, q, dy, dx):
+        ref = part(kind, chip_at(pz, dy, dx))
+        group = POLICY if kind == "p" else SPREAD
+        launch(group, ref, ref, z_recv.at[q, 0], z_mate(1))
+
     def z_in(q, t, count):
         await_bytes(some_rows(count), z_recv.at[q, plane(t)])
 
@@ -288,11 +298,6 @@
             z_in(2, t, block)
         chain_each(t, lambda copy: copy.start())
 
-    spread("c", 8, pz)
-    z_out("c", 0, chip)
-    await_bytes(anc.at[1], anc_sem.at[1])
-    anc_send[...] = anc[1].astype(jnp.bfloat16)
-    launch(SWAP, anc_send, weights.at[1, own_rows, :], anc_sem.at[2], mate)
     for j in range(2, len(pieces)):
         load(j)
     for j, key in enumerate(pieces):
@@ -333,22 +338,25 @@
         else:
             keep_b[i, dx] = total[low:]
 
-    def send_b(i):
-        launch(REDUCE, send_b1.at[i], recv_b1.at[i], rs_recv.at[1, i], y_mate)
-
-    def send_a(i):
-        launch(REDUCE, send_a1.at[i], recv_a1.at[i], rs_recv.at[0, i], x_mate)
+    def send_b(*at):
+        launch(REDUCE, send_b1.at[at], recv_b1.at[at], rs_recv.at[1, at[0]], y_mate)
+
+    def send_a(*at):
+        launch(REDUCE, send_a1.at[at], recv_a1.at[at], rs_recv.at[0, at[0]], x_mate)
 
     def stage_one(i, hold=False):
         first((i, 1))
         block_gradient(i, 1, 1)
+        if not hold:
+            send_a(i, 1)
+            send_b(i, 1)
         block_gradient(i, 1, 0)
         if not hold:
-            send_b(i)
+            send_b(i, 0)
         first((i, 0))
         block_gradient(i, 0, 1)
         if not hold:
-            send_a(i)
+            send_a(i, 0)
         block_gradient(i, 0, 0)
 
     def stage_two(i):
@@ -373,7 +381,7 @@
             launch(REDUCE, send_z.at[i], recv_z.at[pz], rs_recv.at[4, 0], z_mate(3 - i))
 
     def anchor_spread(t):
-        z_in(1, t, block - EARLY)
+        z_in(1, t, block)
         spread("a", t, plane(t))
 
     def anchor_relay(t):
@@ -382,25 +390,26 @@
     stage_one(0)
     stage_one(1)
     stage_one(2, hold=True)
-    relay("c", 8, pz)
-    z_out("c", 0, chip_at(pz, 0, 1))
     stage_two(0)
     send_b(2)
     send_a(2)
+    await_bytes(some_rows(2 * block, 1), xy_recv.at[0, 0])
+    beside("a", 0, 0, 1)
     stage_one(3, hold=True)
     stage_two(1)
     stage_three(0)
-    anchor_relay(0)
+    beside("a", 0, 1, 0)
+    forward("a", 0, pz)
     stage_two(2)
     send_b(3)
     send_a(3)
     stage_three(1)
-    anchor_spread(1)
+    anchor_spread(2)
     stage_three(2)
-    z_out("c", 0, chip_at(pz, 1, 0))
+    relayed("a", 0)
+    beside("a", 0, 1, 1)
     stage_two(3)
-    anchor_spread(2)
-    anchor_relay(1)
+    anchor_relay(2)
     await_bytes(par, own_sem.at[1])
     await_bytes(recv_z.at[pl.ds(0, PLANES - 1)], rs_recv.at[4, 0])
     stage_three(3)
@@ -419,41 +428,39 @@
     spread("p", 4, pz)
 
     tile = tokens_own
-    scale = readout[core]
+    scale = readout[core] * LOG2E
+    blend_scale = scale * blend_rate
+    anchor_scale = scale * (1.0 - blend_rate)
 
     def score_sum(values):
         low_part = jnp.minimum(values, 0.0).reshape(LEN // 8, 8, half)
-        factor = (1.0 + jnp.exp(-jnp.abs(values))).reshape(LEN // 8, 8, half)
+        factor = (1.0 + jnp.exp2(-jnp.abs(values))).reshape(LEN // 8, 8, half)
         product = factor[0]
         for j in range(1, LEN // 8):
             product = product * factor[j]
-        return jnp.sum(low_part, axis=0) - jnp.log(product)
-
-    def multiply(m, t):
-        where = pl.ds(pl.multiple_of(plane(t) * span, span), span)
+        return jnp.sum(low_part, axis=0) - jnp.log2(product)
+
+    def multiply(m, zz, t):
+        where = pl.ds(pl.multiple_of(zz * span, span), span)
 
         @pl.loop(0, 2)
         def _(i):
             value = jnp.dot(
                 tok[i, :, where], weights[m, where, :], preferred_element_type=jnp.float32
             )
-            acc[m, i] = value if t == 0 else acc[m, i] + value
+            value = value if t == 0 else acc[m, i] + value
+            acc[m, i] = value * anchor_scale if m == 1 and t == PLANES - 1 else value
 
     def anchor_multiply(t):
-        relayed("a", t)
-        if t > 0:
-            z_in(0, t, 4 * EARLY)
-        multiply(1, t)
-
-    def policy_multiply(t):
-        relayed("p", 4 + t)
-        multiply(0, t)
-
-    def policy_spread(t):
-        spread("p", 4 + t, plane(t))
-
-    def policy_relay(t):
-        relay("p", 4 + t, plane(t))
+        if t == 1:
+            z_in(1, 1, block)
+            await_bytes(some_rows(3 * block), z_recv.at[0, 0])
+        elif t > 1:
+            relayed("a", t)
+        multiply(1, plane(t), t)
+
+    first_plane = jnp.where(middle, plane(2), plane(3))
+    last_plane = jnp.where(middle, plane(3), plane(2))
 
     def spot(zz, dy, dx):
         return pl.ds(pl.multiple_of(chip_at(zz, dy, dx) * block, block), block)
@@ -477,7 +484,7 @@
             value = acc[0, i] + jnp.dot(
                 tok[i, :, where], weights[0, where, :], preferred_element_type=jnp.float32
             )
-            acc[1, i] = (blend_rate * value + (1.0 - blend_rate) * acc[1, i]) * scale
+            acc[1, i] = value * blend_scale + acc[1, i]
             acc[0, i] = value * scale
             for j in range(tile // LEN):
                 gap = score_sum(acc[0, i, j * LEN : (j + 1) * LEN]) - score_sum(
@@ -486,52 +493,58 @@
                 gap = jnp.sum(gap, axis=0, keepdims=True)
                 gap = jnp.sum(gap, axis=1, keepdims=True)
                 table[me, pl.ds(i * (tile // LEN) + j, 1), :] = jnp.broadcast_to(
-                    gap * (1.0 / LEN), (1, 128)
+                    gap * (1.0 / (LEN * LOG2E)), (1, 128)
                 )
 
     pltpu.make_async_copy(result.at[core], gradient_out.at[:, mine], out_sem.at[0]).start()
     launch(REDUCE, result.at[1 - core], gradient_out.at[:, mine], out_sem.at[0], mate)
 
     anchor_spread(3)
-    relayed("c", 8)
     anchor_multiply(0)
-    anchor_relay(2)
-    policy_relay(0)
-    chain_step(1)
+    relay("p", 4, pz)
 
     @pl.when(middle)
     def _():
+        chain_step(1)
         chain_step(2)
 
-    policy_spread(1)
-    z_out("c", 0, chip_at(pz, 1, 1))
+    beside("p", 3, 0, 1)
+    beside("p", 3, 1, 0)
+    anchor_multiply(2)
     anchor_relay(3)
-    policy_multiply(0)
+    pl.when(jnp.logical_not(middle))(lambda: chain_step(3))
+    spread("p", 5, first_plane)
+    relayed("p", 4)
+    beside("p", 3, 1, 1)
+    multiply(0, pz, 0)
+
+    @pl.when(middle)
+    def _():
+        chain_step(3)
 
     @pl.when(jnp.logical_not(middle))
     def _():
         chain_step(2)
 
-    chain_step(3)
-    policy_spread(2)
-    policy_relay(1)
-    policy_spread(3)
+    spread("p", 6, last_plane)
     anchor_multiply(1)
-    anchor_multiply(2)
-    policy_relay(2)
+    relay("p", 5, first_plane)
     anchor_multiply(3)
-    policy_multiply(1)
-    policy_relay(3)
-    compute_near(plane(3))
-    policy_multiply(2)
+    relay("p", 6, last_plane)
+    relayed("p", 5)
+    multiply(0, first_plane, 2)
+    pl.when(jnp.logical_not(middle))(lambda: chain_step(1))
+    await_bytes(some_rows(3 * block), z_recv.at[3, 0])
+    multiply(0, plane(1), 1)
+    compute_near(last_plane)
     await_bytes(gradient_out, out_sem.at[0])
     await_bytes(tok.at[0], sent_sem.at[TOKENS])
     for group in (SWAP, REDUCE, SPREAD, POLICY):
         await_bytes(some_rows(sent[group]), sent_sem.at[group])
     pl.when(middle)(lambda: await_bytes(some_rows(4 * block), sent_sem.at[CHAIN]))
     pl.when(jnp.logical_not(middle))(lambda: await_bytes(some_rows(2 * block), sent_sem.at[CHAIN]))
-    relayed("p", 7)
-    compute_last(plane(3))
+    relayed("p", 6)
+    compute_last(last_plane)
 
     everyone = [
         (t, dy, dx, dc) for t in (3, 2, 1, 0) for dy, dx, dc in itertools.product((1, 0), repeat=3)
@@ -626,8 +639,8 @@
             dma((8,)),
             dma((3,)),
             dma((5, 4)),
-            dma((9, 2)),
-            dma((3, 4)),
+            dma((7, 2)),
+            dma((4, 4)),
             dma((2,)),
             dma((7,)),
         ],

time: 69.5 us -> 68.1 us (0.980)
  Pallas kernels: 68.7 us -> 67.3 us
    pallas_call x1, Pallas kernels: 66.2 us -> 64.8 us  [fused_shards(): pl.pallas_call(functools.partial(fused_kernel, sizes), out_shape=(weight,...]
where the time goes in v4:
time: 68.1 us; the launch traced here: 67.9 us
  Pallas kernels  67.3 us (99%)
    pallas_call x1, Pallas kernels, fused_shards(): pl.pallas_call(functools.partial(fused_kernel, sizes), out_shape=(weight,...  64.8 us
    pallas_call x1, Pallas kernels, fused_shards(): pl.pallas_call(finish_kernel, out_shape=(weight,) * 4 + (losses,), in_spe...  2.45 us

profile of v4, /device:TPU:0, one launch (start us, length us, event | category | flops | bytes accessed | tf_op | source)
XLA Modules:
  0.0 67.9 jit_solution(7337907903259294311)
XLA Ops:
  0.6 64.8 %shard_map.128 = (f32[128,512]{1,0:T(8,128)}, f32[2]{0:T(128)}) custom-call(bf16[768,4096]{1,0:T(8,128)(2,1)} %tokens.1, bf16[768,512]{1,0:T(8,128)(2,1)} %cotangent.1, f32[128,512]{1,0:T(8,128)} %policy.3, f32[128,512]{1,0:T(8,128)} %anchor.3, f32[128,512]{1,0:T(8,128)} %moment.3, f32[128,512]{1,0:T(8,128)} %second.3, f32[2,1,256]{2,1,0:T(1,128)} %bitcast.1, ...), custom_call_target="tpu_custom_call" | custom-call | tf_op jit(solution)/shard_map/pallas_call | solution.py:609
  65.5 2.5 %shard_map.129 = (f32[128,512]{1,0:T(8,128)}, f32[128,512]{1,0:T(8,128)}, f32[128,512]{1,0:T(8,128)}, f32[128,512]{1,0:T(8,128)}, f32[2]{0:T(128)}) custom-call(f32[128,512]{1,0:T(8,128)} %get-tuple-element.7.gradient, f32[128,512]{1,0:T(8,128)} %policy.3, f32[128,512]{1,0:T(8,128)} %anchor.3, f32[128,512]{1,0:T(8,128)} %moment.3, f32[128,512]{1,0:T(8,128)} %second.3, ...), custom_call_target="tpu_custom_call" | custom-call | tf_op jit(solution)/shard_map/pallas_call | solution.py:661

commit v5 on v4

--- a/solution.py
+++ b/solution.py
@@ -608,7 +608,7 @@
     losses = jax.ShapeDtypeStruct(noisy_flags.shape, f32)
     gradient, loss = pl.pallas_call(
         functools.partial(fused_kernel, sizes),
-        out_shape=(weight, losses),
+        out_shape=(pltpu.VMEM((rows, channels), f32), losses),
         in_specs=[hbm] * 6 + [whole] + [smem] * 2,
         out_specs=(hbm, smem),
         scratch_shapes=[
@@ -663,7 +663,7 @@
         out_shape=(weight,) * 4 + (losses,),
         in_specs=[whole] * 5 + [smem],
         out_specs=(whole,) * 4 + (smem,),
-    )(gradient, policy, anchor, moment, second, loss)
+    )(*(pltpu.with_memory_space_constraint(x, pltpu.VMEM) for x in (gradient, policy, anchor, moment, second)), loss)
     return (policy_next, anchor_next, moment_next, second_next, pair_loss)
 
 

time: 68.1 us -> 67.5 us (level)
  no operation moved by 1% of the time
where the time goes in v5:
time: 67.5 us; the launch traced here: 67.4 us
  Pallas kernels  66.7 us (99%)
  between operations  0.71 us (1%)
    pallas_call x1, Pallas kernels, fused_shards(): pl.pallas_call(functools.partial(fused_kernel, sizes), out_shape=(pltpu.V...  64.8 us
    pallas_call x1, Pallas kernels, fused_shards(): pl.pallas_call(finish_kernel, out_shape=(weight,) * 4 + (losses,), in_spe...  1.84 us

profile of v5, /device:TPU:0, one launch (start us, length us, event | category | flops | bytes accessed | tf_op | source)
XLA Modules:
  0.0 67.4 jit_solution(16722435255632417032)
XLA Ops:
  0.6 0.0 copy-start.3
  0.6 0.0 copy-start.2
  0.7 0.0 copy-start.1
  0.7 0.0 copy-start
  0.7 64.8 %shard_map.128 = (f32[128,512]{1,0:T(8,128)S(1)}, f32[2]{0:T(128)}) custom-call(bf16[768,4096]{1,0:T(8,128)(2,1)} %tokens.1, bf16[768,512]{1,0:T(8,128)(2,1)} %cotangent.1, f32[128,512]{1,0:T(8,128)} %policy.3, f32[128,512]{1,0:T(8,128)} %anchor.3, f32[128,512]{1,0:T(8,128)} %moment.3, f32[128,512]{1,0:T(8,128)} %second.3, f32[2,1,256]{2,1,0:T(1,128)} %bitcast.1, ...), custom_call_target="tpu_custom_call" | custom-call | tf_op jit(solution)/shard_map/pallas_call | solution.py:609
  65.5 0.0 copy-done.3
  65.5 0.0 copy-done.2
  65.5 0.0 copy-done.1
  65.5 0.0 copy-done
  65.5 1.8 %shard_map.129 = (f32[128,512]{1,0:T(8,128)}, f32[128,512]{1,0:T(8,128)}, f32[128,512]{1,0:T(8,128)}, f32[128,512]{1,0:T(8,128)}, f32[2]{0:T(128)}) custom-call(f32[128,512]{1,0:T(8,128)S(1)} %get-tuple-element.7.gradient, f32[128,512]{1,0:T(8,128)S(1)} %copy-done, f32[128,512]{1,0:T(8,128)S(1)} %copy-done.1, f32[128,512]{1,0:T(8,128)S(1)} %copy-done.2, ...), custom_call_target="tpu_custom_call" | custom-call | tf_op jit(solution)/shard_map/pallas_call | solution.py:661
Async XLA Ops:
  0.6 64.9 %copy-start.3 = (f32[128,512]{1,0:T(8,128)S(1)}, f32[128,512]{1,0:T(8,128)}, u32[]{:S(2)}) copy-start(f32[128,512]{1,0:T(8,128)} %second.3) | copy-start | bytes 786436
  0.6 64.9 %copy-start.2 = (f32[128,512]{1,0:T(8,128)S(1)}, f32[128,512]{1,0:T(8,128)}, u32[]{:S(2)}) copy-start(f32[128,512]{1,0:T(8,128)} %moment.3) | copy-start | bytes 786436
  0.7 64.9 %copy-start.1 = (f32[128,512]{1,0:T(8,128)S(1)}, f32[128,512]{1,0:T(8,128)}, u32[]{:S(2)}) copy-start(f32[128,512]{1,0:T(8,128)} %anchor.3) | copy-start | bytes 786436
  0.7 64.9 %copy-start = (f32[128,512]{1,0:T(8,128)S(1)}, f32[128,512]{1,0:T(8,128)}, u32[]{:S(2)}) copy-start(f32[128,512]{1,0:T(8,128)} %policy.3) | copy-start | bytes 786436

commit v6 on v5

--- a/solution.py
+++ b/solution.py
@@ -235,6 +235,8 @@
     kinds = {
         "a": (1, 0, block),
         "p": (0, 0, block),
+        "u": (0, 0, rows),
+        "v": (0, rows, rows),
     }
 
     def part(kind, k, which=None):
@@ -249,7 +251,7 @@
 
     def spread(kind, q, zz):
         ref = part(kind, chip_at(zz, 0, 0))
-        group = POLICY if kind == "p" else SPREAD
+        group = SPREAD if kind == "a" else POLICY
         launch(group, ref, ref, xy_recv.at[q, 0], x_mate)
         launch(group, ref, ref, xy_recv.at[q, 0], y_mate)
 
@@ -258,7 +260,7 @@
         forward(kind, q, zz)
 
     def forward(kind, q, zz):
-        group = POLICY if kind == "p" else SPREAD
+        group = SPREAD if kind == "a" else POLICY
         ref = part(kind, chip_at(zz, 1, 0), 0)
         launch(group, ref, ref, xy_recv.at[q, 1], x_mate)
         ref = part(kind, chip_at(zz, 0, 1), 1)
@@ -274,29 +276,30 @@
 
     def beside(kind, q, dy, dx):
         ref = part(kind, chip_at(pz, dy, dx))
-        group = POLICY if kind == "p" else SPREAD
+        group = SPREAD if kind == "a" else POLICY
         launch(group, ref, ref, z_recv.at[q, 0], z_mate(1))
 
     def z_in(q, t, count):
         await_bytes(some_rows(count), z_recv.at[q, plane(t)])
 
-    def chain_each(t, act):
+    def chain_start(kind, q, t):
         zz = plane(t)
-        ref = part("p", chip_at(zz, 0, 0))
+        ref = part(kind, chip_at(zz, 0, 0))
 
         def to(device):
-            act(remote(ref, ref, sent_sem.at[CHAIN], z_recv.at[2, zz], device))
-
-        if t < PLANES - 1:
-            pl.when(jnp.logical_and(zz <= pz, pz < PLANES - 1))(lambda: to((me + 8) % n))
-            pl.when(jnp.logical_and(zz >= pz, pz > 0))(lambda: to((me + n - 8) % n))
-        if t == 0:
-            pl.when(jnp.logical_not(middle))(lambda: to(z_mate(3)))
-
-    def chain_step(t):
-        if t > 0:
-            z_in(2, t, block)
-        chain_each(t, lambda copy: copy.start())
+            remote(ref, ref, sent_sem.at[CHAIN], z_recv.at[q, zz], device).start()
+
+        pl.when(jnp.logical_and(zz <= pz, pz < PLANES - 1))(lambda: to((me + 8) % n))
+        pl.when(jnp.logical_and(zz >= pz, pz > 0))(lambda: to((me + n - 8) % n))
+
+    def far_start(kind, q):
+        ref = part(kind, chip)
+        remote(ref, ref, sent_sem.at[CHAIN], z_recv.at[q, pz], z_mate(3)).start()
+
+    def chain_wait(*ts):
+        for t in ts:
+            z_in(2, t, rows)
+            z_in(4, t, rows)
 
     for j in range(2, len(pieces)):
         load(j)
@@ -398,7 +401,6 @@
     stage_one(3, hold=True)
     stage_two(1)
     stage_three(0)
-    beside("a", 0, 1, 0)
     forward("a", 0, pz)
     stage_two(2)
     send_b(3)
@@ -406,6 +408,7 @@
     stage_three(1)
     anchor_spread(2)
     stage_three(2)
+    beside("a", 0, 1, 0)
     relayed("a", 0)
     beside("a", 0, 1, 1)
     stage_two(3)
@@ -424,8 +427,16 @@
         weights[0, pl.ds(pl.multiple_of(home + r * rows, rows), rows), :] = updated.astype(
             jnp.bfloat16
         )
-    chain_step(0)
-    spread("p", 4, pz)
+    chain_start("u", 2, 0)
+    chain_start("v", 4, 0)
+
+    @pl.when(jnp.logical_not(middle))
+    def _():
+        far_start("u", 2)
+        far_start("v", 4)
+
+    spread("u", 4, pz)
+    spread("v", 7, pz)
 
     tile = tokens_own
     scale = readout[core] * LOG2E
@@ -501,42 +512,40 @@
 
     anchor_spread(3)
     anchor_multiply(0)
-    relay("p", 4, pz)
-
-    @pl.when(middle)
-    def _():
-        chain_step(1)
-        chain_step(2)
+    for kind, q, chain_q in (("u", 4, 2), ("v", 7, 4)):
+        relay(kind, q, pz)
+
+        @pl.when(middle)
+        def _():
+            for t in (1, 2):
+                z_in(chain_q, t, rows)
+                chain_start(kind, chain_q, t)
 
     beside("p", 3, 0, 1)
     beside("p", 3, 1, 0)
     anchor_multiply(2)
     anchor_relay(3)
-    pl.when(jnp.logical_not(middle))(lambda: chain_step(3))
+    pl.when(jnp.logical_not(middle))(lambda: chain_wait(3))
     spread("p", 5, first_plane)
-    relayed("p", 4)
+    relayed("u", 4)
+    relayed("v", 7)
     beside("p", 3, 1, 1)
     multiply(0, pz, 0)
 
-    @pl.when(middle)
-    def _():
-        chain_step(3)
-
-    @pl.when(jnp.logical_not(middle))
-    def _():
-        chain_step(2)
+    pl.when(middle)(lambda: chain_wait(3))
+    pl.when(jnp.logical_not(middle))(lambda: chain_wait(2))
 
     spread("p", 6, last_plane)
     anchor_multiply(1)
     relay("p", 5, first_plane)
     anchor_multiply(3)
     relay("p", 6, last_plane)
+    compute_near(last_plane)
     relayed("p", 5)
     multiply(0, first_plane, 2)
-    pl.when(jnp.logical_not(middle))(lambda: chain_step(1))
+    pl.when(jnp.logical_not(middle))(lambda: chain_wait(1))
     await_bytes(some_rows(3 * block), z_recv.at[3, 0])
     multiply(0, plane(1), 1)
-    compute_near(last_plane)
     await_bytes(gradient_out, out_sem.at[0])
     await_bytes(tok.at[0], sent_sem.at[TOKENS])
     for group in (SWAP, REDUCE, SPREAD, POLICY):
@@ -639,8 +648,8 @@
             dma((8,)),
             dma((3,)),
             dma((5, 4)),
-            dma((7, 2)),
-            dma((4, 4)),
+            dma((8, 2)),
+            dma((5, 4)),
             dma((2,)),
             dma((7,)),
         ],

time: 67.5 us -> 66.5 us (0.985)
  Pallas kernels: 66.7 us -> 65.6 us
    pallas_call x1, Pallas kernels: 64.8 us -> 63.8 us  [fused_shards(): pl.pallas_call(functools.partial(fused_kernel, sizes), out_shape=(pltpu.V...]
where the time goes in v6:
time: 66.5 us; the launch traced here: 66.4 us
  Pallas kernels  65.6 us (99%)
  between operations  0.71 us (1%)
    pallas_call x1, Pallas kernels, fused_shards(): pl.pallas_call(functools.partial(fused_kernel, sizes), out_shape=(pltpu.V...  63.8 us
    pallas_call x1, Pallas kernels, fused_shards(): pl.pallas_call(finish_kernel, out_shape=(weight,) * 4 + (losses,), in_spe...  1.84 us

profile of v6, /device:TPU:0, one launch (start us, length us, event | category | flops | bytes accessed | tf_op | source)
XLA Modules:
  0.0 66.4 jit_solution(11146169763857530361)
XLA Ops:
  0.6 0.0 copy-start.3
  0.6 0.0 copy-start.2
  0.7 0.0 copy-start.1
  0.7 0.0 copy-start
  0.7 63.8 %shard_map.128 = (f32[128,512]{1,0:T(8,128)S(1)}, f32[2]{0:T(128)}) custom-call(bf16[768,4096]{1,0:T(8,128)(2,1)} %tokens.1, bf16[768,512]{1,0:T(8,128)(2,1)} %cotangent.1, f32[128,512]{1,0:T(8,128)} %policy.3, f32[128,512]{1,0:T(8,128)} %anchor.3, f32[128,512]{1,0:T(8,128)} %moment.3, f32[128,512]{1,0:T(8,128)} %second.3, f32[2,1,256]{2,1,0:T(1,128)} %bitcast.1, ...), custom_call_target="tpu_custom_call" | custom-call | tf_op jit(solution)/shard_map/pallas_call | solution.py:618
  64.5 0.0 copy-done.3
  64.5 0.0 copy-done.2
  64.5 0.0 copy-done.1
  64.5 0.0 copy-done
  64.5 1.8 %shard_map.129 = (f32[128,512]{1,0:T(8,128)}, f32[128,512]{1,0:T(8,128)}, f32[128,512]{1,0:T(8,128)}, f32[128,512]{1,0:T(8,128)}, f32[2]{0:T(128)}) custom-call(f32[128,512]{1,0:T(8,128)S(1)} %get-tuple-element.7.gradient, f32[128,512]{1,0:T(8,128)S(1)} %copy-done, f32[128,512]{1,0:T(8,128)S(1)} %copy-done.1, f32[128,512]{1,0:T(8,128)S(1)} %copy-done.2, ...), custom_call_target="tpu_custom_call" | custom-call | tf_op jit(solution)/shard_map/pallas_call | solution.py:670
Async XLA Ops:
  0.6 63.8 %copy-start.3 = (f32[128,512]{1,0:T(8,128)S(1)}, f32[128,512]{1,0:T(8,128)}, u32[]{:S(2)}) copy-start(f32[128,512]{1,0:T(8,128)} %second.3) | copy-start | bytes 786436
  0.6 63.8 %copy-start.2 = (f32[128,512]{1,0:T(8,128)S(1)}, f32[128,512]{1,0:T(8,128)}, u32[]{:S(2)}) copy-start(f32[128,512]{1,0:T(8,128)} %moment.3) | copy-start | bytes 786436
  0.7 63.8 %copy-start.1 = (f32[128,512]{1,0:T(8,128)S(1)}, f32[128,512]{1,0:T(8,128)}, u32[]{:S(2)}) copy-start(f32[128,512]{1,0:T(8,128)} %anchor.3) | copy-start | bytes 786436
  0.7 63.8 %copy-start = (f32[128,512]{1,0:T(8,128)S(1)}, f32[128,512]{1,0:T(8,128)}, u32[]{:S(2)}) copy-start(f32[128,512]{1,0:T(8,128)} %policy.3) | copy-start | bytes 786436

commit v7 on v6

--- a/solution.py
+++ b/solution.py
@@ -274,8 +274,8 @@
             ref = part(kind, k)
             launch(SPREAD, ref, ref, z_recv.at[q, pz], z_mate(t))
 
-    def beside(kind, q, dy, dx):
-        ref = part(kind, chip_at(pz, dy, dx))
+    def beside(kind, q, dy, dx, which=None):
+        ref = part(kind, chip_at(pz, dy, dx), which)
         group = SPREAD if kind == "a" else POLICY
         launch(group, ref, ref, z_recv.at[q, 0], z_mate(1))
 
@@ -398,6 +398,7 @@
     send_a(2)
     await_bytes(some_rows(2 * block, 1), xy_recv.at[0, 0])
     beside("a", 0, 0, 1)
+    beside("a", 0, 1, 0, 0)
     stage_one(3, hold=True)
     stage_two(1)
     stage_three(0)
@@ -408,7 +409,7 @@
     stage_three(1)
     anchor_spread(2)
     stage_three(2)
-    beside("a", 0, 1, 0)
+    beside("a", 0, 1, 0, 1)
     relayed("a", 0)
     beside("a", 0, 1, 1)
     stage_two(3)

time: 66.5 us -> 66.4 us (level)
  no operation moved by 1% of the time
where the time goes in v7:
time: 66.4 us; the launch traced here: 66.3 us
  Pallas kernels  65.5 us (99%)
  between operations  0.71 us (1%)
    pallas_call x1, Pallas kernels, fused_shards(): pl.pallas_call(functools.partial(fused_kernel, sizes), out_shape=(pltpu.V...  63.7 us
    pallas_call x1, Pallas kernels, fused_shards(): pl.pallas_call(finish_kernel, out_shape=(weight,) * 4 + (losses,), in_spe...  1.84 us

profile of v7, /device:TPU:0, one launch (start us, length us, event | category | flops | bytes accessed | tf_op | source)
XLA Modules:
  0.0 66.3 jit_solution(10093190419333102397)
XLA Ops:
  0.6 0.0 copy-start.3
  0.6 0.0 copy-start.2
  0.7 0.0 copy-start.1
  0.7 0.0 copy-start
  0.7 63.7 %shard_map.128 = (f32[128,512]{1,0:T(8,128)S(1)}, f32[2]{0:T(128)}) custom-call(bf16[768,4096]{1,0:T(8,128)(2,1)} %tokens.1, bf16[768,512]{1,0:T(8,128)(2,1)} %cotangent.1, f32[128,512]{1,0:T(8,128)} %policy.3, f32[128,512]{1,0:T(8,128)} %anchor.3, f32[128,512]{1,0:T(8,128)} %moment.3, f32[128,512]{1,0:T(8,128)} %second.3, f32[2,1,256]{2,1,0:T(1,128)} %bitcast.1, ...), custom_call_target="tpu_custom_call" | custom-call | tf_op jit(solution)/shard_map/pallas_call | solution.py:619
  64.4 0.0 copy-done.3
  64.4 0.0 copy-done.2
  64.4 0.0 copy-done.1
  64.4 0.0 copy-done
  64.4 1.8 %shard_map.129 = (f32[128,512]{1,0:T(8,128)}, f32[128,512]{1,0:T(8,128)}, f32[128,512]{1,0:T(8,128)}, f32[128,512]{1,0:T(8,128)}, f32[2]{0:T(128)}) custom-call(f32[128,512]{1,0:T(8,128)S(1)} %get-tuple-element.7.gradient, f32[128,512]{1,0:T(8,128)S(1)} %copy-done, f32[128,512]{1,0:T(8,128)S(1)} %copy-done.1, f32[128,512]{1,0:T(8,128)S(1)} %copy-done.2, ...), custom_call_target="tpu_custom_call" | custom-call | tf_op jit(solution)/shard_map/pallas_call | solution.py:671
Async XLA Ops:
  0.6 63.7 %copy-start.3 = (f32[128,512]{1,0:T(8,128)S(1)}, f32[128,512]{1,0:T(8,128)}, u32[]{:S(2)}) copy-start(f32[128,512]{1,0:T(8,128)} %second.3) | copy-start | bytes 786436
  0.6 63.7 %copy-start.2 = (f32[128,512]{1,0:T(8,128)S(1)}, f32[128,512]{1,0:T(8,128)}, u32[]{:S(2)}) copy-start(f32[128,512]{1,0:T(8,128)} %moment.3) | copy-start | bytes 786436
  0.7 63.7 %copy-start.1 = (f32[128,512]{1,0:T(8,128)S(1)}, f32[128,512]{1,0:T(8,128)}, u32[]{:S(2)}) copy-start(f32[128,512]{1,0:T(8,128)} %anchor.3) | copy-start | bytes 786436
  0.7 63.7 %copy-start = (f32[128,512]{1,0:T(8,128)S(1)}, f32[128,512]{1,0:T(8,128)}, u32[]{:S(2)}) copy-start(f32[128,512]{1,0:T(8,128)} %policy.3) | copy-start | bytes 786436
